TPU v7x, 32 devices: a whole 2x2x4 slice. The times are simulated.
32 devices in a mesh: dp: 16 (over z, y, core), fsdp: 2 (over x).
Axes of the slice: x: 2, y: 2, z: 4, core: 2. Of those that a mesh axis runs over, the one named last changes fastest.
Arguments:
- text_states: bfloat16 [256, 128, 768], P(('dp', 'fsdp')), may hold values from -6 to 6
- image_states: bfloat16 [64, 36, 1024], P(('dp', 'fsdp')), may hold values from -6 to 6
- text_lengths: int32 [256], P(('dp', 'fsdp')), may hold values from 8 to 128, as said below
- region_mask: int32 [64, 36], P(('dp', 'fsdp')), may hold values from 0 to 1, as said below
- group_ids: int32 [256], P(('dp', 'fsdp')), may hold values from 0 to 63, as said below
- image_query: bfloat16 [1024, 1024], P('dp', 'fsdp'), may hold values from -0.1875 to 0.1875
- image_key: bfloat16 [1024, 1024], P('dp', 'fsdp'), may hold values from -0.1875 to 0.1875
- image_value: bfloat16 [1024, 1024], P('dp', 'fsdp'), may hold values from -0.1875 to 0.1875
- text_query: bfloat16 [768, 1024], P('dp', 'fsdp'), may hold values from -0.21875 to 0.21875
- text_key: bfloat16 [768, 1024], P('dp', 'fsdp'), may hold values from -0.21875 to 0.21875
- text_value: bfloat16 [768, 1024], P('dp', 'fsdp'), may hold values from -0.21875 to 0.21875
- image_output: bfloat16 [1024, 1024], P('dp', 'fsdp'), may hold values from -1.5 to 1.5
- text_output: bfloat16 [1024, 768], P('dp', 'fsdp'), may hold values from -0.75 to 0.75
- image_inner: bfloat16 [1024, 1024], P('dp', 'fsdp'), may hold values from -0.1875 to 0.1875
- image_outer: bfloat16 [1024, 1024], P('dp', 'fsdp'), may hold values from -0.1875 to 0.1875
- text_inner: bfloat16 [768, 3072], P('dp', 'fsdp'), may hold values from -0.21875 to 0.21875
- text_outer: bfloat16 [3072, 768], P('dp', 'fsdp'), may hold values from -0.109375 to 0.109375
- norm_params: float32 [4, 1792], P(None, ('dp', 'fsdp')), may hold values from -1.2 to 2, as said below
- cot_text: bfloat16 [256, 128, 768], P(('dp', 'fsdp')), may hold values from -6 to 6
- cot_image: bfloat16 [256, 36, 1024], P(('dp', 'fsdp')), may hold values from -6 to 6
Outputs:
- text_out: bfloat16 [256, 128, 768], P(('dp', 'fsdp'))
- image_out: bfloat16 [256, 36, 1024], P(('dp', 'fsdp'))
- text_grad: float32 [256, 128, 768], P(('dp', 'fsdp'))
- image_grad: float32 [64, 36, 1024], P(('dp', 'fsdp'))
- image_query_grad: float32 [1024, 1024], P('dp', 'fsdp')
- image_key_grad: float32 [1024, 1024], P('dp', 'fsdp')
- image_value_grad: float32 [1024, 1024], P('dp', 'fsdp')
- text_query_grad: float32 [768, 1024], P('dp', 'fsdp')
- text_key_grad: float32 [768, 1024], P('dp', 'fsdp')
- text_value_grad: float32 [768, 1024], P('dp', 'fsdp')
- image_output_grad: float32 [1024, 1024], P('dp', 'fsdp')
- text_output_grad: float32 [1024, 768], P('dp', 'fsdp')
- image_inner_grad: float32 [1024, 1024], P('dp', 'fsdp')
- image_outer_grad: float32 [1024, 1024], P('dp', 'fsdp')
- text_inner_grad: float32 [768, 3072], P('dp', 'fsdp')
- text_outer_grad: float32 [3072, 768], P('dp', 'fsdp')
- norm_grad: float32 [4, 1792], P(None, ('dp', 'fsdp'))
Inputs may be any that keep to these rules, and one draw needn't show every extreme that they name: `text_lengths`: one pair has exactly 128 tokens and one has 8. `region_mask`: each image's regions fill a leading run of its slots, of 9 to 36 regions; one image has 36, one has 9. `group_ids`: the pairs of each aligned block of 8 pairs name the 2 images of the same block index, each of them exactly four times. `norm_params`: rows 0 and 2 are gains between 0.5 and 2, rows 1 and 3 shifts.
All inputs are finite; a program needn't handle non-finite values.
Results may differ from a plain program's by a relative error of at most 0.019.
Values may be sent and summed in bfloat16 or wider, within the bound.
A program may use at most 192 MiB of HBM per device.

v0:
```python
import math

import jax
import jax.numpy as jnp
from jax import lax
from jax.sharding import PartitionSpec as P

HDIM = 128


norm_eps = 1e-12
masked_score = -1e30


def layer_norm(z, gain, shift):
    centre = jnp.mean(z, axis=-1, keepdims=True)
    offset = z - centre
    spread = jnp.mean(offset * offset, axis=-1, keepdims=True)
    return offset * lax.rsqrt(spread + norm_eps) * gain + shift


def gelu_exact(value):
    return jax.nn.gelu(value, approximate=False)


def project(inputs, matrix):
    return jnp.einsum("bti,io->bto", inputs, matrix, preferred_element_type=jnp.float32)


def project_back(grads, matrix):
    return jnp.einsum("bto,io->bti", grads, matrix, preferred_element_type=jnp.float32)


def weight_grad(inputs, grads):
    return jnp.einsum("bti,bto->io", inputs, grads, preferred_element_type=jnp.float32)


def split_heads(value):
    return value.reshape(value.shape[0], value.shape[1], value.shape[2] // HDIM, HDIM)


def merge_low(value):
    return value.reshape(value.shape[0], value.shape[1], -1).astype(jnp.bfloat16)


def gather_weights(shards):
    wider = (
        lax.all_gather(shards[0], "fsdp", axis=1, tiled=True),
        lax.all_gather(shards[1], "fsdp", axis=1, tiled=True),
        lax.all_gather(shards[2], "fsdp", axis=1, tiled=True),
        lax.all_gather(shards[3], "fsdp", axis=1, tiled=True),
        lax.all_gather(shards[4], "fsdp", axis=1, tiled=True),
        lax.all_gather(shards[5], "fsdp", axis=1, tiled=True),
        lax.all_gather(shards[6], "fsdp", axis=1, tiled=True),
        lax.all_gather(shards[7], "fsdp", axis=1, tiled=True),
        lax.all_gather(shards[8], "fsdp", axis=1, tiled=True),
        lax.all_gather(shards[9], "fsdp", axis=1, tiled=True),
        lax.all_gather(shards[10], "fsdp", axis=1, tiled=True),
        lax.all_gather(shards[11], "fsdp", axis=1, tiled=True),
    )
    return (
        lax.all_gather(wider[0], "dp", axis=0, tiled=True),
        lax.all_gather(wider[1], "dp", axis=0, tiled=True),
        lax.all_gather(wider[2], "dp", axis=0, tiled=True),
        lax.all_gather(wider[3], "dp", axis=0, tiled=True),
        lax.all_gather(wider[4], "dp", axis=0, tiled=True),
        lax.all_gather(wider[5], "dp", axis=0, tiled=True),
        lax.all_gather(wider[6], "dp", axis=0, tiled=True),
        lax.all_gather(wider[7], "dp", axis=0, tiled=True),
        lax.all_gather(wider[8], "dp", axis=0, tiled=True),
        lax.all_gather(wider[9], "dp", axis=0, tiled=True),
        lax.all_gather(wider[10], "dp", axis=0, tiled=True),
        lax.all_gather(wider[11], "dp", axis=0, tiled=True),
    )


def reduce_grads(grads):
    narrow = (
        lax.psum_scatter(
            grads[0].astype(jnp.bfloat16), "dp", scatter_dimension=0, tiled=True
        ).astype(jnp.float32),
        lax.psum_scatter(
            grads[1].astype(jnp.bfloat16), "dp", scatter_dimension=0, tiled=True
        ).astype(jnp.float32),
        lax.psum_scatter(
            grads[2].astype(jnp.bfloat16), "dp", scatter_dimension=0, tiled=True
        ).astype(jnp.float32),
        lax.psum_scatter(
            grads[3].astype(jnp.bfloat16), "dp", scatter_dimension=0, tiled=True
        ).astype(jnp.float32),
        lax.psum_scatter(
            grads[4].astype(jnp.bfloat16), "dp", scatter_dimension=0, tiled=True
        ).astype(jnp.float32),
        lax.psum_scatter(
            grads[5].astype(jnp.bfloat16), "dp", scatter_dimension=0, tiled=True
        ).astype(jnp.float32),
        lax.psum_scatter(
            grads[6].astype(jnp.bfloat16), "dp", scatter_dimension=0, tiled=True
        ).astype(jnp.float32),
        lax.psum_scatter(
            grads[7].astype(jnp.bfloat16), "dp", scatter_dimension=0, tiled=True
        ).astype(jnp.float32),
        lax.psum_scatter(
            grads[8].astype(jnp.bfloat16), "dp", scatter_dimension=0, tiled=True
        ).astype(jnp.float32),
        lax.psum_scatter(
            grads[9].astype(jnp.bfloat16), "dp", scatter_dimension=0, tiled=True
        ).astype(jnp.float32),
        lax.psum_scatter(
            grads[10].astype(jnp.bfloat16), "dp", scatter_dimension=0, tiled=True
        ).astype(jnp.float32),
        lax.psum_scatter(
            grads[11].astype(jnp.bfloat16), "dp", scatter_dimension=0, tiled=True
        ).astype(jnp.float32),
    )
    return (
        lax.psum_scatter(
            narrow[0].astype(jnp.bfloat16), "fsdp", scatter_dimension=1, tiled=True
        ).astype(jnp.float32),
        lax.psum_scatter(
            narrow[1].astype(jnp.bfloat16), "fsdp", scatter_dimension=1, tiled=True
        ).astype(jnp.float32),
        lax.psum_scatter(
            narrow[2].astype(jnp.bfloat16), "fsdp", scatter_dimension=1, tiled=True
        ).astype(jnp.float32),
        lax.psum_scatter(
            narrow[3].astype(jnp.bfloat16), "fsdp", scatter_dimension=1, tiled=True
        ).astype(jnp.float32),
        lax.psum_scatter(
            narrow[4].astype(jnp.bfloat16), "fsdp", scatter_dimension=1, tiled=True
        ).astype(jnp.float32),
        lax.psum_scatter(
            narrow[5].astype(jnp.bfloat16), "fsdp", scatter_dimension=1, tiled=True
        ).astype(jnp.float32),
        lax.psum_scatter(
            narrow[6].astype(jnp.bfloat16), "fsdp", scatter_dimension=1, tiled=True
        ).astype(jnp.float32),
        lax.psum_scatter(
            narrow[7].astype(jnp.bfloat16), "fsdp", scatter_dimension=1, tiled=True
        ).astype(jnp.float32),
        lax.psum_scatter(
            narrow[8].astype(jnp.bfloat16), "fsdp", scatter_dimension=1, tiled=True
        ).astype(jnp.float32),
        lax.psum_scatter(
            narrow[9].astype(jnp.bfloat16), "fsdp", scatter_dimension=1, tiled=True
        ).astype(jnp.float32),
        lax.psum_scatter(
            narrow[10].astype(jnp.bfloat16), "fsdp", scatter_dimension=1, tiled=True
        ).astype(jnp.float32),
        lax.psum_scatter(
            narrow[11].astype(jnp.bfloat16), "fsdp", scatter_dimension=1, tiled=True
        ).astype(jnp.float32),
    )


def stream_forward(resid, context, w_out, w_inner, w_outer, norms, keep):
    branch = project(context, w_out)
    mid, first_back = jax.vjp(layer_norm, resid + branch, norms[0], norms[1])
    mid_low = mid.astype(jnp.bfloat16)
    hidden = project(mid_low, w_inner)
    act = gelu_exact(hidden).astype(jnp.bfloat16)
    ffn = project(act, w_outer)

    def closing(total, gain, shift):
        return layer_norm(total, gain, shift) * keep[..., None]

    result, second_back = jax.vjp(closing, mid + ffn, norms[2], norms[3])
    return (result, (first_back, second_back, mid_low, hidden, act))


def stream_backward(cotangent, kept, context, w_out, w_inner, w_outer):
    first_back, second_back, mid_low, hidden, act = kept
    second_dz, second_gain, second_shift = second_back(cotangent)
    ffn_low = second_dz.astype(jnp.bfloat16)
    outer_grad = weight_grad(act, ffn_low)
    act_grad = project_back(ffn_low, w_outer)
    hidden_grad = jax.vjp(gelu_exact, hidden)[1](act_grad)[0]
    hidden_low = hidden_grad.astype(jnp.bfloat16)
    inner_grad = weight_grad(mid_low, hidden_low)
    mid_grad = second_dz + project_back(hidden_low, w_inner)
    first_dz, first_gain, first_shift = first_back(mid_grad)
    branch_low = first_dz.astype(jnp.bfloat16)
    out_grad = weight_grad(context, branch_low)
    context_grad = project_back(branch_low, w_out).astype(jnp.bfloat16)
    return (
        first_dz,
        context_grad,
        (out_grad, inner_grad, outer_grad),
        (first_gain, first_shift, second_gain, second_shift),
    )


def body(
    text_states,
    image_states,
    text_lengths,
    region_mask,
    group_ids,
    image_query,
    image_key,
    image_value,
    text_query,
    text_key,
    text_value,
    image_output,
    text_output,
    image_inner,
    image_outer,
    text_inner,
    text_outer,
    norm_params,
    cot_text,
    cot_image,
):
    shards = (
        image_query,
        image_key,
        image_value,
        text_query,
        text_key,
        text_value,
        image_output,
        text_output,
        image_inner,
        image_outer,
        text_inner,
        text_outer,
    )
    weights = gather_weights(shards)
    norms = lax.all_gather(norm_params, ("dp", "fsdp"), axis=1, tiled=True)
    width_text = text_states.shape[2]
    images = image_states.shape[0]
    length = text_states.shape[1]
    device = lax.axis_index("dp") * lax.axis_size("fsdp") + lax.axis_index("fsdp")
    local = group_ids - device * images
    visual = jnp.take(image_states, local, axis=0)
    text_keep = (jnp.arange(length, dtype=jnp.int32)[None, :] < text_lengths[:, None]).astype(
        jnp.float32
    )
    region_keep = jnp.take(region_mask, local, axis=0).astype(jnp.float32)
    scale = 1.0 / math.sqrt(HDIM)
    (
        query_image,
        key_image,
        value_image,
        query_text,
        key_text,
        value_text,
        out_image,
        out_text,
        inner_image,
        outer_image,
        inner_text,
        outer_text,
    ) = weights
    image_queries = split_heads(project(visual, query_image).astype(jnp.bfloat16))
    image_keys = split_heads(project(visual, key_image).astype(jnp.bfloat16))
    image_values = split_heads(project(visual, value_image).astype(jnp.bfloat16))
    text_queries = split_heads(project(text_states, query_text).astype(jnp.bfloat16))
    text_keys = split_heads(project(text_states, key_text).astype(jnp.bfloat16))
    text_values = split_heads(project(text_states, value_text).astype(jnp.bfloat16))
    image_scores = scale * jnp.einsum(
        "brhe,blhe->bhrl", image_queries, text_keys, preferred_element_type=jnp.float32
    )
    image_scores = jnp.where(text_keep[:, None, None, :] > 0, image_scores, masked_score)
    image_probs = jax.nn.softmax(image_scores, axis=3)
    image_low = image_probs.astype(jnp.bfloat16)
    image_context = merge_low(
        jnp.einsum("bhrl,blhe->brhe", image_low, text_values, preferred_element_type=jnp.float32)
    )
    text_scores = scale * jnp.einsum(
        "brhe,blhe->bhrl", image_keys, text_queries, preferred_element_type=jnp.float32
    )
    text_scores = jnp.where(region_keep[:, None, :, None] > 0, text_scores, masked_score)
    text_probs = jax.nn.softmax(text_scores, axis=2)
    text_low = text_probs.astype(jnp.bfloat16)
    text_context = merge_low(
        jnp.einsum("bhrl,brhe->blhe", text_low, image_values, preferred_element_type=jnp.float32)
    )
    text_result, text_kept = stream_forward(
        text_states.astype(jnp.float32),
        text_context,
        out_text,
        inner_text,
        outer_text,
        norms[:, :width_text],
        text_keep,
    )
    image_result, image_kept = stream_forward(
        visual.astype(jnp.float32),
        image_context,
        out_image,
        inner_image,
        outer_image,
        norms[:, width_text:],
        region_keep,
    )
    weights = gather_weights(shards)
    (
        query_image,
        key_image,
        value_image,
        query_text,
        key_text,
        value_text,
        out_image,
        out_text,
        inner_image,
        outer_image,
        inner_text,
        outer_text,
    ) = weights
    text_dz, text_dcontext, text_wgrads, text_ngrads = stream_backward(
        cot_text.astype(jnp.float32), text_kept, text_context, out_text, inner_text, outer_text
    )
    image_dz, image_dcontext, image_wgrads, image_ngrads = stream_backward(
        cot_image.astype(jnp.float32),
        image_kept,
        image_context,
        out_image,
        inner_image,
        outer_image,
    )
    image_ctx_grad = split_heads(image_dcontext)
    text_ctx_grad = split_heads(text_dcontext)
    image_dprobs = jnp.einsum(
        "brhe,blhe->bhrl", image_ctx_grad, text_values, preferred_element_type=jnp.float32
    )
    text_values_grad = jnp.einsum(
        "bhrl,brhe->blhe", image_low, image_ctx_grad, preferred_element_type=jnp.float32
    )
    image_dscores = (
        image_probs * (image_dprobs - jnp.sum(image_probs * image_dprobs, axis=3, keepdims=True))
    ).astype(jnp.bfloat16)
    image_queries_grad = scale * jnp.einsum(
        "bhrl,blhe->brhe", image_dscores, text_keys, preferred_element_type=jnp.float32
    )
    text_keys_grad = scale * jnp.einsum(
        "bhrl,brhe->blhe", image_dscores, image_queries, preferred_element_type=jnp.float32
    )
    text_dprobs = jnp.einsum(
        "blhe,brhe->bhrl", text_ctx_grad, image_values, preferred_element_type=jnp.float32
    )
    image_values_grad = jnp.einsum(
        "bhrl,blhe->brhe", text_low, text_ctx_grad, preferred_element_type=jnp.float32
    )
    text_dscores = (
        text_probs * (text_dprobs - jnp.sum(text_probs * text_dprobs, axis=2, keepdims=True))
    ).astype(jnp.bfloat16)
    text_queries_grad = scale * jnp.einsum(
        "bhrl,brhe->blhe", text_dscores, image_keys, preferred_element_type=jnp.float32
    )
    image_keys_grad = scale * jnp.einsum(
        "bhrl,blhe->brhe", text_dscores, text_queries, preferred_element_type=jnp.float32
    )
    image_query_low = merge_low(image_queries_grad)
    image_key_low = merge_low(image_keys_grad)
    image_value_low = merge_low(image_values_grad)
    text_query_low = merge_low(text_queries_grad)
    text_key_low = merge_low(text_keys_grad)
    text_value_low = merge_low(text_values_grad)
    visual_grad = (
        image_dz
        + project_back(image_query_low, query_image)
        + project_back(image_key_low, key_image)
    )
    visual_grad = visual_grad + project_back(image_value_low, value_image)
    selector = (local[:, None] == jnp.arange(images, dtype=jnp.int32)[None, :]).astype(jnp.float32)
    image_grad = jnp.einsum("pi,prd->ird", selector, visual_grad, precision=lax.Precision.HIGHEST)
    text_grad = (
        text_dz + project_back(text_query_low, query_text) + project_back(text_key_low, key_text)
    )
    text_grad = text_grad + project_back(text_value_low, value_text)
    local_grads = (
        weight_grad(visual, image_query_low),
        weight_grad(visual, image_key_low),
        weight_grad(visual, image_value_low),
        weight_grad(text_states, text_query_low),
        weight_grad(text_states, text_key_low),
        weight_grad(text_states, text_value_low),
        image_wgrads[0],
        text_wgrads[0],
        image_wgrads[1],
        image_wgrads[2],
        text_wgrads[1],
        text_wgrads[2],
    )
    owned = reduce_grads(local_grads)
    norm_rows = jnp.stack(
        [
            jnp.concatenate([text_ngrads[0], image_ngrads[0]]),
            jnp.concatenate([text_ngrads[1], image_ngrads[1]]),
            jnp.concatenate([text_ngrads[2], image_ngrads[2]]),
            jnp.concatenate([text_ngrads[3], image_ngrads[3]]),
        ]
    )
    norm_grad = lax.psum_scatter(norm_rows, ("dp", "fsdp"), scatter_dimension=1, tiled=True)
    return (
        text_result.astype(jnp.bfloat16),
        image_result.astype(jnp.bfloat16),
        text_grad,
        image_grad,
        owned[0],
        owned[1],
        owned[2],
        owned[3],
        owned[4],
        owned[5],
        owned[6],
        owned[7],
        owned[8],
        owned[9],
        owned[10],
        owned[11],
        norm_grad,
    )


def solution(mesh):
    placed = (
        P(("dp", "fsdp"), None, None),
        P(("dp", "fsdp"), None, None),
        P(("dp", "fsdp")),
        P(("dp", "fsdp"), None),
        P(("dp", "fsdp")),
        P("dp", "fsdp"),
        P("dp", "fsdp"),
        P("dp", "fsdp"),
        P("dp", "fsdp"),
        P("dp", "fsdp"),
        P("dp", "fsdp"),
        P("dp", "fsdp"),
        P("dp", "fsdp"),
        P("dp", "fsdp"),
        P("dp", "fsdp"),
        P("dp", "fsdp"),
        P("dp", "fsdp"),
        P(None, ("dp", "fsdp")),
        P(("dp", "fsdp"), None, None),
        P(("dp", "fsdp"), None, None),
    )
    return jax.shard_map(
        body,
        mesh=mesh,
        in_specs=placed,
        out_specs=(
            P(("dp", "fsdp"), None, None),
            P(("dp", "fsdp"), None, None),
            P(("dp", "fsdp"), None, None),
            P(("dp", "fsdp"), None, None),
            P("dp", "fsdp"),
            P("dp", "fsdp"),
            P("dp", "fsdp"),
            P("dp", "fsdp"),
            P("dp", "fsdp"),
            P("dp", "fsdp"),
            P("dp", "fsdp"),
            P("dp", "fsdp"),
            P("dp", "fsdp"),
            P("dp", "fsdp"),
            P("dp", "fsdp"),
            P("dp", "fsdp"),
            P(None, ("dp", "fsdp")),
        ),
        check_vma=False,
    )
```

profile of v0, /device:TPU:0, one launch (start us, length us, event | category | flops | bytes accessed | tf_op | source)
XLA Modules:
  0.0 1503.7 jit_solution(13180635335929339480)
XLA Ops:
  7.3 7.5 all_gather.116
  14.9 5.1 all_gather.112
  20.0 6.1 all_gather.114
  26.2 5.3 all_gather.118
  31.6 6.6 all_gather.120
  38.2 5.6 all_gather.122
  43.9 5.6 all_gather.103
  49.6 5.0 all_gather.101
  62.5 65.2 %all-gather = f32[32,56,4]{1,2,0:T(4,128)S(1)} all-gather(f32[1,56,4]{1,2,0:T(4,128)S(1)} %bitcast.316), channel_id=1, replica_groups=mesh['dp'=16,'fsdp'=2] {'dp','fsdp'}, dimensions={0}, use_global_device_ids=true | all-gather | bytes 29568 | tf_op jit(solution)/shard_map/all_gather | solution.py:230
  144.7 10.8 fusion.214
  155.5 7.0 fusion.163
  166.7 14.1 all-gather.32.cloned.1.call-done
  184.4 38.6 %all-gather.34.cloned.1.call-done = bf16[1024,1024]{1,0:T(8,128)(2,1)} async-done(((bf16[64,1024]{1,0:T(8,128)(2,1)}), bf16[1024,1024]{1,0:T(8,128)(2,1)}) %all-gather.34.cloned.1.call-update) | async-done | bytes 2097168 | tf_op jit(solution)/shard_map/all_gather | solution.py:70
  231.2 34.0 %all-gather.36.cloned.1.call-done = bf16[1024,1024]{1,0:T(8,128)(2,1)} async-done(((bf16[64,1024]{1,0:T(8,128)(2,1)}), bf16[1024,1024]{1,0:T(8,128)(2,1)}) %all-gather.36.cloned.1.call-update) | async-done | bytes 2097168 | tf_op jit(solution)/shard_map/all_gather | solution.py:71
  283.2 8.4 convolution_convert_fusion
  335.2 5.9 all_gather.108
  341.2 5.9 all_gather.110
  354.9 35.9 %all-gather.14.cloned.1.call-done = bf16[1024,1024]{1,0:T(8,128)(2,1)} async-done(((bf16[64,1024]{1,0:T(8,128)(2,1)}), bf16[1024,1024]{1,0:T(8,128)(2,1)}) %all-gather.14.cloned.1.call-update) | async-done | bytes 2097168 | tf_op jit(solution)/shard_map/all_gather | solution.py:64
  393.9 58.7 %reduce-scatter.78.cloned.1.call-done = bf16[48,1024]{1,0:T(8,128)(2,1)} async-done(((bf16[768,1024]{1,0:T(8,128)(2,1)}), bf16[48,1024]{1,0:T(8,128)(2,1)}) %reduce-scatter.78.cloned.1.call-update) | async-done | bytes 98320
  457.6 57.7 %reduce-scatter.76.cloned.1.call-done = bf16[48,1024]{1,0:T(8,128)(2,1)} async-done(((bf16[768,1024]{1,0:T(8,128)(2,1)}), bf16[48,1024]{1,0:T(8,128)(2,1)}) %reduce-scatter.76.cloned.1.call-update) | async-done | bytes 98320
  518.4 61.1 %reduce-scatter.64.cloned.1.call-done = bf16[64,1024]{1,0:T(8,128)(2,1)} async-done(((bf16[1024,1024]{1,0:T(8,128)(2,1)}), bf16[64,1024]{1,0:T(8,128)(2,1)}) %reduce-scatter.64.cloned.1.call-update) | async-done | bytes 131088 | tf_op jit(solution)/shard_map/reduce_scatter | solution.py:106
  581.8 62.4 %reduce-scatter.60.cloned.1.call-done = bf16[64,1024]{1,0:T(8,128)(2,1)} async-done(((bf16[1024,1024]{1,0:T(8,128)(2,1)}), bf16[64,1024]{1,0:T(8,128)(2,1)}) %reduce-scatter.60.cloned.1.call-update) | async-done | bytes 131088 | tf_op jit(solution)/shard_map/reduce_scatter | solution.py:103
  644.5 40.6 %all-gather.20.cloned.1.call-done = bf16[1024,768]{1,0:T(8,128)(2,1)} async-done(((bf16[64,768]{1,0:T(8,128)(2,1)}), bf16[1024,768]{1,0:T(8,128)(2,1)}) %all-gather.20.cloned.1.call-update) | async-done | bytes 1572880 | tf_op jit(solution)/shard_map/all_gather | solution.py:69
  689.7 59.5 %reduce-scatter.54.cloned.1.call-done = bf16[64,1024]{1,0:T(8,128)(2,1)} async-done(((bf16[1024,1024]{1,0:T(8,128)(2,1)}), bf16[64,1024]{1,0:T(8,128)(2,1)}) %reduce-scatter.54.cloned.1.call-update) | async-done | bytes 131088 | tf_op jit(solution)/shard_map/reduce_scatter | solution.py:97
  749.7 64.7 %reduce-scatter.36.cloned.1.call-done = bf16[64,1024]{1,0:T(8,128)(2,1)} async-done(((bf16[1024,1024]{1,0:T(8,128)(2,1)}), bf16[64,1024]{1,0:T(8,128)(2,1)}) %reduce-scatter.36.cloned.1.call-update) | async-done | bytes 131088 | tf_op jit(solution)/shard_map/reduce_scatter | solution.py:79
  814.5 54.5 %all-gather.22.cloned.1.call-done = bf16[768,3072]{1,0:T(8,128)(2,1)} async-done(((bf16[48,3072]{1,0:T(8,128)(2,1)}), bf16[768,3072]{1,0:T(8,128)(2,1)}) %all-gather.22.cloned.1.call-update) | async-done | bytes 4718608 | tf_op jit(solution)/shard_map/all_gather | solution.py:72
  869.0 10.4 fusion.18
  883.8 29.6 %multiply_convert_fusion = (bf16[8,128,3072]{2,1,0:T(8,128)(2,1)}, f32[8,128,3072]{2,1,0:T(8,128)}) fusion(f32[8,128,3072]{2,1,0:T(8,128)S(1)} %get-tuple-element.120, u8[128,3072]{1,0:T(8,128)(4,1)S(1)} %get-tuple-element.69, u8[128,3072]{1,0:T(8,128)(4,1)S(1)} %get-tuple-element.68), kind=kLoop, calls=%fused_computation.12 | loop fusion | flops 220200960 | bytes 32243712 | tf_op jit(solution)/shard_map/convert_element_type | solution.py:161
  913.5 9.7 all-gather.24.cloned.1.call-done
  923.1 9.0 fusion.213
  936.9 17.0 %add_convert_fusion = bf16[8,128,3072]{2,1,0:T(8,128)(2,1)} fusion(f32[8,128,3072]{2,1,0:T(8,128)} %get-tuple-element.99, f32[8,128,3072]{2,1,0:T(8,128)} %copy-done.2, bf16[3072,768]{1,0:T(8,128)(2,1)} %all-gather.24.cloned.1.call-done, f32[8,128]{1,0:T(8,128)S(1)} %negate_multiply_fusion.5, bf16[8,128,768]{2,1,0:T(8,128)(2,1)} %param.38, ...), kind=kOutput, calls=%fused_computation.11 | convolution fusion | flops 4883742720 | bytes 40918016 | tf_op jit(solution)/shard_map/bto,io->bti/dot_general | solution.py:31
  953.9 11.1 multiply_reduce_fusion.1
  1008.5 12.5 bitcast_convert_fusion
  1021.0 10.0 bitcast_convert_fusion.1
  1049.9 13.7 reduce-scatter.58.cloned.1.call-done
  1065.6 60.5 %reduce-scatter.74.cloned.1.call-done = bf16[48,1024]{1,0:T(8,128)(2,1)} async-done(((bf16[768,1024]{1,0:T(8,128)(2,1)}), bf16[48,1024]{1,0:T(8,128)(2,1)}) %reduce-scatter.74.cloned.1.call-update) | async-done | bytes 98320
  1130.8 59.5 %reduce-scatter.44.cloned.1.call-done = bf16[64,1024]{1,0:T(8,128)(2,1)} async-done(((bf16[1024,1024]{1,0:T(8,128)(2,1)}), bf16[64,1024]{1,0:T(8,128)(2,1)}) %reduce-scatter.44.cloned.1.call-update) | async-done | bytes 131088 | tf_op jit(solution)/shard_map/reduce_scatter | solution.py:85
  1192.8 62.3 %reduce-scatter.40.cloned.1.call-done = bf16[64,1024]{1,0:T(8,128)(2,1)} async-done(((bf16[1024,1024]{1,0:T(8,128)(2,1)}), bf16[64,1024]{1,0:T(8,128)(2,1)}) %reduce-scatter.40.cloned.1.call-update) | async-done | bytes 131088 | tf_op jit(solution)/shard_map/reduce_scatter | solution.py:82
  1257.2 76.3 %reduce-scatter.72.cloned.1.call-done = bf16[192,768]{1,0:T(8,128)(2,1)} async-done(((bf16[3072,768]{1,0:T(8,128)(2,1)}), bf16[192,768]{1,0:T(8,128)(2,1)}) %reduce-scatter.72.cloned.1.call-update) | async-done | bytes 294928 | tf_op jit(solution)/shard_map/reduce_scatter | solution.py:112
  1335.5 40.2 %all-reduce = f32[4,1792]{1,0:T(4,128)S(1)} all-reduce(f32[4,1792]{1,0:T(4,128)S(1)} %pad_maximum_fusion), channel_id=26, replica_groups=mesh['dp'=16,'fsdp'=2] {'dp','fsdp'}, use_global_device_ids=true, to_apply=%region_54.55.clone | all-reduce | flops 7168 | bytes 57344
  1376.4 5.7 fusion.82
  1382.1 30.9 %reduce-scatter.68.cloned.1.call-done = bf16[48,3072]{1,0:T(8,128)(2,1)} async-done(((bf16[768,3072]{1,0:T(8,128)(2,1)}), bf16[48,3072]{1,0:T(8,128)(2,1)}) %reduce-scatter.68.cloned.1.call-update) | async-done | bytes 294928 | tf_op jit(solution)/shard_map/reduce_scatter | solution.py:109
  1413.1 7.9 add_add_fusion.2
  1427.5 12.9 reduce-scatter.48.cloned.1.call-done
  1442.0 10.8 reduce-scatter.46.cloned.1.call-done
  1454.3 11.1 reduce-scatter.42.cloned.1.call-done
  1466.9 14.0 reduce-scatter.82.cloned.1.call-done
  1482.7 12.3 reduce-scatter.70.cloned.1.call-done
  (344 shorter events, 228.6 us)
Async XLA Ops:
  7.2 53.2 %copy-start = (bf16[2,36,1024]{2,0,1:T(2,128)(2,1)S(1)}, bf16[2,36,1024]{2,0,1:T(2,128)(2,1)}, u32[]{:S(2)}) copy-start(bf16[2,36,1024]{2,0,1:T(2,128)(2,1)} %param.21) | copy-start | bytes 442372
  7.2 52.6 %copy-start.60 = (s32[8]{0:T(128)S(1)}, s32[8]{0:T(128)}, u32[]{:S(2)}) copy-start(s32[8]{0:T(128)} %param.24) | copy-start | bytes 100
  7.2 120.8 %all-gather.30.cloned.1.call-start = ((), (), s32[]{:S(2)}) async-start(), calls=%async_computation.32 | async-start | bytes 1671168 | tf_op jit(solution)/shard_map/all_gather | solution.py:66
  14.8 117.7 %all-gather.26.cloned.1.call-start = ((), (), s32[]{:S(2)}) async-start(), calls=%async_computation.30 | async-start | bytes 1671168 | tf_op jit(solution)/shard_map/all_gather | solution.py:67
  20.0 118.5 %all-gather.28.cloned.1.call-start = ((), (), s32[]{:S(2)}) async-start(), calls=%async_computation.31 | async-start | bytes 2228224 | tf_op jit(solution)/shard_map/all_gather | solution.py:62
  26.1 154.7 %all-gather.32.cloned.1.call-start = ((), (), s32[]{:S(2)}) async-start(), calls=%async_computation.33 | async-start | bytes 2228224 | tf_op jit(solution)/shard_map/all_gather | solution.py:68
  31.5 191.5 %all-gather.34.cloned.1.call-start = ((), (), s32[]{:S(2)}) async-start(), calls=%async_computation.34 | async-start | bytes 2228224 | tf_op jit(solution)/shard_map/all_gather | solution.py:70
  38.2 227.0 %all-gather.36.cloned.1.call-start = ((), (), s32[]{:S(2)}) async-start(), calls=%async_computation.35 | async-start | bytes 2228224 | tf_op jit(solution)/shard_map/all_gather | solution.py:71
  43.8 303.4 %all-gather.18.cloned.1.call-start = ((), (), s32[]{:S(2)}) async-start(), calls=%async_computation.26 | async-start | bytes 1671168 | tf_op jit(solution)/shard_map/all_gather | solution.py:65
  49.5 302.3 %all-gather.16.cloned.1.call-start = ((), (), s32[]{:S(2)}) async-start(), calls=%async_computation.25 | async-start | bytes 2228224 | tf_op jit(solution)/shard_map/all_gather | solution.py:63
  54.6 336.2 %all-gather.14.cloned.1.call-start = ((), (), s32[]{:S(2)}) async-start(), calls=%async_computation.24 | async-start | bytes 2228224 | tf_op jit(solution)/shard_map/all_gather | solution.py:64
  59.8 392.8 %reduce-scatter.78.cloned.1.call-start = ((), (), s32[]{:S(2)}) async-start(), calls=%async_computation.57 | async-start | bytes 1671168
  60.4 67.4 %copy-start.61 = (s32[8]{0:T(128)S(1)}, s32[8]{0:T(128)}, u32[]{:S(2)}) copy-start(s32[8]{0:T(128)} %param.22) | copy-start | bytes 100
  60.4 67.6 %copy-start.29 = (bf16[8,128,768]{2,1,0:T(8,128)(2,1)S(1)}, bf16[8,128,768]{2,1,0:T(8,128)(2,1)}, u32[]{:S(2)}) copy-start(bf16[8,128,768]{2,1,0:T(8,128)(2,1)} %param.20) | copy-start | bytes 4718596
  61.9 76.5 %copy-start.37 = (bf16[8,36,1024]{2,0,1:T(8,128)(2,1)}, bf16[8,36,1024]{2,0,1:T(8,128)(2,1)S(1)}, u32[]{:S(2)}) copy-start(bf16[8,36,1024]{2,0,1:T(8,128)(2,1)S(1)} %gather_fusion) | copy-start | bytes 1769476
  299.3 216.0 %reduce-scatter.76.cloned.1.call-start = ((), (), s32[]{:S(2)}) async-start(), calls=%async_computation.56 | async-start | bytes 1671168
  311.5 268.0 %reduce-scatter.64.cloned.1.call-start = ((), (), s32[]{:S(2)}) async-start(), calls=%async_computation.50 | async-start | bytes 2228224 | tf_op jit(solution)/shard_map/reduce_scatter | solution.py:106
  315.9 328.4 %reduce-scatter.60.cloned.1.call-start = ((), (), s32[]{:S(2)}) async-start(), calls=%async_computation.48 | async-start | bytes 2228224 | tf_op jit(solution)/shard_map/reduce_scatter | solution.py:103
  319.7 365.4 %all-gather.20.cloned.1.call-start = ((), (), s32[]{:S(2)}) async-start(), calls=%async_computation.27 | async-start | bytes 1671168 | tf_op jit(solution)/shard_map/all_gather | solution.py:69
  325.4 423.8 %reduce-scatter.54.cloned.1.call-start = ((), (), s32[]{:S(2)}) async-start(), calls=%async_computation.45 | async-start | bytes 2228224 | tf_op jit(solution)/shard_map/reduce_scatter | solution.py:97
  328.4 486.1 %reduce-scatter.36.cloned.1.call-start = ((), (), s32[]{:S(2)}) async-start(), calls=%async_computation.36 | async-start | bytes 2228224 | tf_op jit(solution)/shard_map/reduce_scatter | solution.py:79
  334.3 534.7 %all-gather.22.cloned.1.call-start = ((), (), s32[]{:S(2)}) async-start(), calls=%async_computation.28 | async-start | bytes 5013504 | tf_op jit(solution)/shard_map/all_gather | solution.py:72
  341.1 582.0 %all-gather.24.cloned.1.call-start = ((), (), s32[]{:S(2)}) async-start(), calls=%async_computation.29 | async-start | bytes 5013504 | tf_op jit(solution)/shard_map/all_gather | solution.py:73
  347.1 693.4 %reduce-scatter.52.cloned.1.call-start = ((), (), s32[]{:S(2)}) async-start(), calls=%async_computation.44 | async-start | bytes 393216 | tf_op jit(solution)/shard_map/reduce_scatter | solution.py:132
  354.9 99.5 %copy-start.5 = (bf16[8,36,8,128]{3,2,1,0:T(8,128)(2,1)}, bf16[8,36,8,128]{3,2,1,0:T(8,128)(2,1)S(1)}, u32[]{:S(2)}) copy-start(bf16[8,36,8,128]{3,2,1,0:T(8,128)(2,1)S(1)} %reshape.343) | copy-start | bytes 1769476
  393.9 185.7 %copy-start.43 = (bf16[8,36,8,128]{3,2,1,0:T(8,128)(2,1)}, bf16[8,36,8,128]{3,2,1,0:T(8,128)(2,1)S(1)}, u32[]{:S(2)}) copy-start(bf16[8,36,8,128]{3,2,1,0:T(8,128)(2,1)S(1)} %reshape.342) | copy-start | bytes 1769476
  454.4 587.9 %reduce-scatter.50.cloned.1.call-start = ((), (), s32[]{:S(2)}) async-start(), calls=%async_computation.43 | async-start | bytes 393216 | tf_op jit(solution)/shard_map/reduce_scatter | solution.py:129
  457.6 124.3 %copy-start.9 = (f32[8,8,36,128]{3,2,1,0:T(8,128)}, f32[8,8,36,128]{3,2,1,0:T(8,128)S(1)}, u32[]{:S(2)}) copy-start(f32[8,8,36,128]{3,2,1,0:T(8,128)S(1)} %fusion.123) | copy-start | bytes 3538948
  517.0 526.9 %reduce-scatter.66.cloned.1.call-start = ((), (), s32[]{:S(2)}) async-start(), calls=%async_computation.51 | async-start | bytes 196608 | tf_op jit(solution)/shard_map/reduce_scatter | solution.py:144
  579.5 465.9 %reduce-scatter.62.cloned.1.call-start = ((), (), s32[]{:S(2)}) async-start(), calls=%async_computation.49 | async-start | bytes 196608 | tf_op jit(solution)/shard_map/reduce_scatter | solution.py:141
  644.3 402.6 %reduce-scatter.56.cloned.1.call-start = ((), (), s32[]{:S(2)}) async-start(), calls=%async_computation.46 | async-start | bytes 196608 | tf_op jit(solution)/shard_map/reduce_scatter | solution.py:135
  749.2 299.2 %reduce-scatter.38.cloned.1.call-start = ((), (), s32[]{:S(2)}) async-start(), calls=%async_computation.37 | async-start | bytes 196608 | tf_op jit(solution)/shard_map/reduce_scatter | solution.py:117
  814.5 249.2 %reduce-scatter.58.cloned.1.call-start = ((), (), s32[]{:S(2)}) async-start(), calls=%async_computation.47 | async-start | bytes 1671168 | tf_op jit(solution)/shard_map/reduce_scatter | solution.py:100
  971.6 154.5 %reduce-scatter.74.cloned.1.call-start = ((), (), s32[]{:S(2)}) async-start(), calls=%async_computation.55 | async-start | bytes 1671168
  986.3 204.0 %reduce-scatter.44.cloned.1.call-start = ((), (), s32[]{:S(2)}) async-start(), calls=%async_computation.40 | async-start | bytes 2228224 | tf_op jit(solution)/shard_map/reduce_scatter | solution.py:85
  998.5 256.6 %reduce-scatter.40.cloned.1.call-start = ((), (), s32[]{:S(2)}) async-start(), calls=%async_computation.38 | async-start | bytes 2228224 | tf_op jit(solution)/shard_map/reduce_scatter | solution.py:82
  1008.4 325.1 %reduce-scatter.72.cloned.1.call-start = ((), (), s32[]{:S(2)}) async-start(), calls=%async_computation.54 | async-start | bytes 5013504 | tf_op jit(solution)/shard_map/reduce_scatter | solution.py:112
  1021.0 392.1 %reduce-scatter.68.cloned.1.call-start = ((), (), s32[]{:S(2)}) async-start(), calls=%async_computation.52 | async-start | bytes 5013504 | tf_op jit(solution)/shard_map/reduce_scatter | solution.py:109
  1031.0 394.9 %reduce-scatter.80.cloned.1.call-start = ((), (), s32[]{:S(2)}) async-start(), calls=%async_computation.58 | async-start | bytes 294912
  1040.6 87.3 %copy-start.21 = (bf16[8,36,1024]{2,1,0:T(8,128)(2,1)S(1)}, bf16[8,36,1024]{2,1,0:T(8,128)(2,1)}, u32[]{:S(2)}) copy-start(bf16[8,36,1024]{2,1,0:T(8,128)(2,1)} %reshape.359) | copy-start | bytes 1769476
  1065.4 375.0 %reduce-scatter.48.cloned.1.call-start = ((), (), s32[]{:S(2)}) async-start(), calls=%async_computation.42 | async-start | bytes 393216 | tf_op jit(solution)/shard_map/reduce_scatter | solution.py:126
  1127.8 62.5 %copy-start.20 = (bf16[8,36,1024]{2,1,0:T(8,128)(2,1)S(1)}, bf16[8,36,1024]{2,1,0:T(8,128)(2,1)}, u32[]{:S(2)}) copy-start(bf16[8,36,1024]{2,1,0:T(8,128)(2,1)} %reshape.360) | copy-start | bytes 1769476
  1127.8 325.0 %reduce-scatter.46.cloned.1.call-start = ((), (), s32[]{:S(2)}) async-start(), calls=%async_computation.41 | async-start | bytes 196608 | tf_op jit(solution)/shard_map/reduce_scatter | solution.py:123
  1190.3 64.9 %copy-start.58 = (s32[8]{0:T(128)S(1)}, s32[8]{0:T(128)}, u32[]{:S(2)}) copy-start(s32[8]{0:T(128)} %copy-done.57) | copy-start | bytes 100
  1190.3 275.1 %reduce-scatter.42.cloned.1.call-start = ((), (), s32[]{:S(2)}) async-start(), calls=%async_computation.39 | async-start | bytes 196608 | tf_op jit(solution)/shard_map/reduce_scatter | solution.py:120
  1255.1 225.7 %reduce-scatter.82.cloned.1.call-start = ((), (), s32[]{:S(2)}) async-start(), calls=%async_computation.59 | async-start | bytes 589824
  1335.4 159.6 %reduce-scatter.70.cloned.1.call-start = ((), (), s32[]{:S(2)}) async-start(), calls=%async_computation.53 | async-start | bytes 442368 | tf_op jit(solution)/shard_map/reduce_scatter | solution.py:147
  1413.1 83.6 %copy-start.1 = (bf16[2,36,1024]{2,0,1:T(2,128)(2,1)S(1)}, bf16[2,36,1024]{2,0,1:T(2,128)(2,1)}, u32[]{:S(2)}) copy-start(bf16[2,36,1024]{2,0,1:T(2,128)(2,1)} %param.21) | copy-start | bytes 442372
  (57 other events, 399.6 us)
Sparse Core Ops, SparseCore 0:
  14.9 40.0 all-gather.29
  57.3 38.5 all-gather.25
  98.1 40.2 all-gather.27
  140.5 40.2 all-gather.31
  182.8 40.1 all-gather.33
  225.0 40.1 all-gather.35
  267.5 38.4 all-gather.17
  308.1 40.2 all-gather.15
  350.6 40.1 all-gather.13
  394.3 58.2 reduce-scatter.77
  456.7 58.4 reduce-scatter.75
  518.8 60.5 reduce-scatter.63
  583.7 60.5 reduce-scatter.59
  646.4 38.6 all-gather.19
  688.7 60.4 reduce-scatter.53
  753.8 60.5 reduce-scatter.35
  816.6 52.3 all-gather.21
  871.1 51.9 all-gather.23
  925.9 10.1 reduce-scatter.51
  938.9 11.6 reduce-scatter.49
  952.8 10.2 reduce-scatter.65
  965.3 10.2 reduce-scatter.61
  977.8 10.2 reduce-scatter.55
  990.2 10.2 reduce-scatter.37
  1004.1 59.4 reduce-scatter.57
  1067.6 58.3 reduce-scatter.73
  1129.6 60.5 reduce-scatter.43
  1194.4 60.6 reduce-scatter.39
  1259.0 74.4 reduce-scatter.71
  1337.7 75.2 reduce-scatter.67
  1415.8 9.9 reduce-scatter.79
  1428.7 11.6 reduce-scatter.47
  1442.5 10.2 reduce-scatter.45
  1455.1 10.2 reduce-scatter.41
  1467.7 13.1 reduce-scatter.81
  1482.9 12.0 reduce-scatter.69
where the time goes:
time: 1510 us; the launch traced here: 1500 us
  waiting for transfers between devices  963 us (64%)
  matrix products  217 us (14%)
  blocking collectives  174 us (12%)
  other arithmetic  69.8 us (5%)
  local copies, waits for them, and re-layouts  61.7 us (4%)
  between operations  15.9 us (1%)
    unnamed x41, waiting for transfers between devices  196 us
    reduce_scatter x1, waiting for transfers between devices, reduce_grads(): lax.psum_scatter(grads[11].astype(jnp.bfloat16), 'dp', scatter_dimension=...  76.3 us
    all_gather x1, blocking collectives, body(): norms = lax.all_gather(norm_params, ('dp', 'fsdp'), axis=1, tiled=True)  65.2 us
    dot_general x12, matrix products, project_back(): jnp.einsum('bto,io->bti', grads, matrix, preferred_element_type=jnp.float32)  65 us
    reduce_scatter x1, waiting for transfers between devices, reduce_grads(): lax.psum_scatter(grads[0].astype(jnp.bfloat16), 'dp', scatter_dimension=0...  64.7 us
    reduce_scatter x1, waiting for transfers between devices, reduce_grads(): lax.psum_scatter(grads[8].astype(jnp.bfloat16), 'dp', scatter_dimension=0...  62.4 us
    reduce_scatter x1, waiting for transfers between devices, reduce_grads(): lax.psum_scatter(grads[1].astype(jnp.bfloat16), 'dp', scatter_dimension=0...  62.3 us
    reduce_scatter x1, waiting for transfers between devices, reduce_grads(): lax.psum_scatter(grads[9].astype(jnp.bfloat16), 'dp', scatter_dimension=0...  61.1 us
  transfers between devices with their start and end apart: 36, of which 26 were waited for; matrix products, arithmetic and copies ran while one was open for 22% of the time, Pallas kernels for 0%

commit v1 on v0

--- a/solution.py
+++ b/solution.py
@@ -1,8 +1,11 @@
+import functools
 import math
 
 import jax
 import jax.numpy as jnp
 from jax import lax
+from jax.experimental import pallas as pl
+from jax.experimental.pallas import tpu as pltpu
 from jax.sharding import PartitionSpec as P
 
 HDIM = 128
@@ -10,6 +13,234 @@
 
 norm_eps = 1e-12
 masked_score = -1e30
+
+MESH_IDS = pl.DeviceIdType.MESH
+
+
+def bits_of(size):
+    count = size.bit_length() - 1
+    assert 1 << count == size
+    return count
+
+
+def hop_orders(nd, nf):
+    high = [("d", b) for b in range(nd - 1, 2, -1)]
+    low = [("d", 2)]
+    near = [("d", 1)]
+    wide = [("f", b) for b in range(nf)]
+    return (
+        high + near + low + wide,
+        low + high + wide + near,
+        high + wide + near + low,
+    )
+
+
+CORE = ("d", 0)
+
+
+class Place:
+    def __init__(self, nd, nf):
+        self.d = lax.axis_index("dp")
+        self.f = lax.axis_index("fsdp")
+        self.axes = [("f", b) for b in range(nf - 1, -1, -1)] + [
+            ("d", b) for b in range(nd - 1, -1, -1)
+        ]
+
+    def bit(self, axis):
+        value = self.f if axis[0] == "f" else self.d
+        return lax.rem(value // (1 << axis[1]), 2)
+
+    def partner(self, axis):
+        step = (1 << axis[1]) * (1 - 2 * self.bit(axis))
+        if axis[0] == "f":
+            return (self.d, self.f + step)
+        return (self.d + step, self.f)
+
+    def index(self, whole, flip=None):
+        picked = []
+        for axis in self.axes:
+            if axis in whole:
+                picked.append(slice(None))
+            elif axis == flip:
+                picked.append(1 - self.bit(axis))
+            else:
+                picked.append(self.bit(axis))
+        return tuple(picked)
+
+    def barrier(self):
+        sem = pltpu.get_barrier_semaphore()
+        for axis in self.axes:
+            pl.semaphore_signal(
+                sem, inc=1, device_id=self.partner(axis), device_id_type=MESH_IDS
+            )
+        pl.semaphore_wait(sem, len(self.axes))
+
+
+def gather_kernel(nd, nf, routes, *refs):
+    count = len(routes)
+    ins, outs = refs[:count], refs[count : 2 * count]
+    local_sem, send_sem, recv_sem = refs[2 * count :]
+    place = Place(nd, nf)
+    local = []
+    for m in range(count):
+        copy = pltpu.make_async_copy(ins[m], outs[m].at[place.index(())], local_sem.at[m])
+        copy.start()
+        local.append(copy)
+    place.barrier()
+    hops = len(routes[0])
+    sent = [[] for _ in range(count)]
+    for h in range(hops):
+        for m in range(count):
+            if h == 0:
+                local[m].wait()
+            else:
+                sent[m][h - 1].wait_recv()
+            region = outs[m].at[place.index(routes[m][:h])]
+            copy = pltpu.make_async_remote_copy(
+                src_ref=region,
+                dst_ref=region,
+                send_sem=send_sem.at[m, h],
+                recv_sem=recv_sem.at[m, h],
+                device_id=place.partner(routes[m][h]),
+                device_id_type=MESH_IDS,
+            )
+            copy.start()
+            sent[m].append(copy)
+    for m in range(count):
+        sent[m][hops - 1].wait_recv()
+        for h in range(hops):
+            sent[m][h].wait_send()
+
+
+def gather_blocks(shards, parts, nd, nf, collective_id):
+    orders = hop_orders(nd, nf)
+    routes = [tuple(orders[part]) + (CORE,) for part in parts]
+    count, hops = len(shards), len(routes[0])
+    lead = (2,) * (nd + nf)
+    return pl.pallas_call(
+        functools.partial(gather_kernel, nd, nf, routes),
+        out_shape=[jax.ShapeDtypeStruct(lead + s.shape, s.dtype) for s in shards],
+        in_specs=[pl.BlockSpec(memory_space=pl.ANY)] * count,
+        out_specs=[pl.BlockSpec(memory_space=pl.ANY)] * count,
+        scratch_shapes=[
+            pltpu.SemaphoreType.DMA((count,)),
+            pltpu.SemaphoreType.DMA((count, hops)),
+            pltpu.SemaphoreType.DMA((count, hops)),
+        ],
+        compiler_params=pltpu.CompilerParams(
+            collective_id=collective_id, has_side_effects=True
+        ),
+    )(*shards)
+
+
+def add_blocks(place, acc, index, incoming, out=None):
+    lead = incoming.shape[:-2]
+    total = math.prod(lead)
+
+    def spot(i):
+        inner = []
+        for size in reversed(lead):
+            inner.append(lax.rem(i, size))
+            i = i // size
+        return tuple(reversed(inner))
+
+    def full(at):
+        at = list(at)
+        return tuple(at.pop(0) if isinstance(p, slice) else p for p in index)
+
+    if out is not None:
+        out[...] = acc[index].astype(jnp.float32) + incoming[...].astype(jnp.float32)
+        return
+
+    def one(i, carry):
+        at = spot(i)
+        where = full(at)
+        acc[where] = acc[where] + incoming[at]
+        return carry
+
+    lax.fori_loop(0, total, one, 0)
+
+
+def reduce_kernel(nd, nf, routes, *refs):
+    count = len(routes)
+    hops = len(routes[0])
+    ins, outs = refs[:count], refs[count : 2 * count]
+    accs = refs[2 * count : 3 * count]
+    temps = [refs[3 * count + m * hops : 3 * count + (m + 1) * hops] for m in range(count)]
+    local_sem, send_sem, recv_sem = refs[3 * count + count * hops :]
+    place = Place(nd, nf)
+    rest = [axis for axis in place.axes if axis != CORE]
+    local = []
+    for m in range(count):
+        copy = pltpu.make_async_copy(ins[m].at[place.index(rest)], accs[m], local_sem.at[m])
+        copy.start()
+        local.append(copy)
+    place.barrier()
+    sent = [[] for _ in range(count)]
+
+    def send(m, h, region):
+        copy = pltpu.make_async_remote_copy(
+            src_ref=region,
+            dst_ref=temps[m][h],
+            send_sem=send_sem.at[m, h],
+            recv_sem=recv_sem.at[m, h],
+            device_id=place.partner(routes[m][h]),
+            device_id_type=MESH_IDS,
+        )
+        copy.start()
+        sent[m].append(copy)
+
+    def within(m, h, flip=None):
+        whole = routes[m][h + 1 :]
+        full = place.index(whole, flip)
+        return tuple(p for p, axis in zip(full, place.axes) if axis != CORE)
+
+    for m in range(count):
+        send(m, 0, ins[m].at[place.index(routes[m][1:], CORE)])
+    for m in range(count):
+        local[m].wait()
+    for h in range(1, hops + 1):
+        for m in range(count):
+            sent[m][h - 1].wait_recv()
+            here = within(m, h - 1)
+            if h == hops:
+                add_blocks(place, accs[m], here, temps[m][h - 1], outs[m])
+            else:
+                add_blocks(place, accs[m], here, temps[m][h - 1])
+                send(m, h, accs[m].at[within(m, h, routes[m][h])])
+    for m in range(count):
+        for h in range(hops):
+            sent[m][h].wait_send()
+
+
+def reduce_blocks(blocks, parts, nd, nf, collective_id):
+    orders = hop_orders(nd, nf)
+    routes = [(CORE,) + tuple(reversed(orders[part])) for part in parts]
+    count, hops = len(blocks), len(routes[0])
+    shapes = [b.shape[-2:] for b in blocks]
+    scratch = [
+        pltpu.VMEM((2,) * (nd + nf - 1) + s, b.dtype) for s, b in zip(shapes, blocks)
+    ]
+    for s, b in zip(shapes, blocks):
+        for h in range(hops):
+            scratch.append(pltpu.VMEM((2,) * (hops - 1 - h) + s, b.dtype))
+    return pl.pallas_call(
+        functools.partial(reduce_kernel, nd, nf, routes),
+        out_shape=[jax.ShapeDtypeStruct(s, jnp.float32) for s in shapes],
+        in_specs=[pl.BlockSpec(memory_space=pl.ANY)] * count,
+        out_specs=[pl.BlockSpec(memory_space=pltpu.VMEM)] * count,
+        scratch_shapes=scratch
+        + [
+            pltpu.SemaphoreType.DMA((count,)),
+            pltpu.SemaphoreType.DMA((count, hops)),
+            pltpu.SemaphoreType.DMA((count, hops)),
+        ],
+        compiler_params=pltpu.CompilerParams(
+            collective_id=collective_id,
+            has_side_effects=True,
+            vmem_limit_bytes=60 * 1024 * 1024,
+        ),
+    )(*blocks)
 
 
 def layer_norm(z, gain, shift):
@@ -43,114 +274,43 @@
     return value.reshape(value.shape[0], value.shape[1], -1).astype(jnp.bfloat16)
 
 
-def gather_weights(shards):
-    wider = (
-        lax.all_gather(shards[0], "fsdp", axis=1, tiled=True),
-        lax.all_gather(shards[1], "fsdp", axis=1, tiled=True),
-        lax.all_gather(shards[2], "fsdp", axis=1, tiled=True),
-        lax.all_gather(shards[3], "fsdp", axis=1, tiled=True),
-        lax.all_gather(shards[4], "fsdp", axis=1, tiled=True),
-        lax.all_gather(shards[5], "fsdp", axis=1, tiled=True),
-        lax.all_gather(shards[6], "fsdp", axis=1, tiled=True),
-        lax.all_gather(shards[7], "fsdp", axis=1, tiled=True),
-        lax.all_gather(shards[8], "fsdp", axis=1, tiled=True),
-        lax.all_gather(shards[9], "fsdp", axis=1, tiled=True),
-        lax.all_gather(shards[10], "fsdp", axis=1, tiled=True),
-        lax.all_gather(shards[11], "fsdp", axis=1, tiled=True),
-    )
-    return (
-        lax.all_gather(wider[0], "dp", axis=0, tiled=True),
-        lax.all_gather(wider[1], "dp", axis=0, tiled=True),
-        lax.all_gather(wider[2], "dp", axis=0, tiled=True),
-        lax.all_gather(wider[3], "dp", axis=0, tiled=True),
-        lax.all_gather(wider[4], "dp", axis=0, tiled=True),
-        lax.all_gather(wider[5], "dp", axis=0, tiled=True),
-        lax.all_gather(wider[6], "dp", axis=0, tiled=True),
-        lax.all_gather(wider[7], "dp", axis=0, tiled=True),
-        lax.all_gather(wider[8], "dp", axis=0, tiled=True),
-        lax.all_gather(wider[9], "dp", axis=0, tiled=True),
-        lax.all_gather(wider[10], "dp", axis=0, tiled=True),
-        lax.all_gather(wider[11], "dp", axis=0, tiled=True),
-    )
-
-
-def reduce_grads(grads):
-    narrow = (
-        lax.psum_scatter(
-            grads[0].astype(jnp.bfloat16), "dp", scatter_dimension=0, tiled=True
-        ).astype(jnp.float32),
-        lax.psum_scatter(
-            grads[1].astype(jnp.bfloat16), "dp", scatter_dimension=0, tiled=True
-        ).astype(jnp.float32),
-        lax.psum_scatter(
-            grads[2].astype(jnp.bfloat16), "dp", scatter_dimension=0, tiled=True
-        ).astype(jnp.float32),
-        lax.psum_scatter(
-            grads[3].astype(jnp.bfloat16), "dp", scatter_dimension=0, tiled=True
-        ).astype(jnp.float32),
-        lax.psum_scatter(
-            grads[4].astype(jnp.bfloat16), "dp", scatter_dimension=0, tiled=True
-        ).astype(jnp.float32),
-        lax.psum_scatter(
-            grads[5].astype(jnp.bfloat16), "dp", scatter_dimension=0, tiled=True
-        ).astype(jnp.float32),
-        lax.psum_scatter(
-            grads[6].astype(jnp.bfloat16), "dp", scatter_dimension=0, tiled=True
-        ).astype(jnp.float32),
-        lax.psum_scatter(
-            grads[7].astype(jnp.bfloat16), "dp", scatter_dimension=0, tiled=True
-        ).astype(jnp.float32),
-        lax.psum_scatter(
-            grads[8].astype(jnp.bfloat16), "dp", scatter_dimension=0, tiled=True
-        ).astype(jnp.float32),
-        lax.psum_scatter(
-            grads[9].astype(jnp.bfloat16), "dp", scatter_dimension=0, tiled=True
-        ).astype(jnp.float32),
-        lax.psum_scatter(
-            grads[10].astype(jnp.bfloat16), "dp", scatter_dimension=0, tiled=True
-        ).astype(jnp.float32),
-        lax.psum_scatter(
-            grads[11].astype(jnp.bfloat16), "dp", scatter_dimension=0, tiled=True
-        ).astype(jnp.float32),
-    )
-    return (
-        lax.psum_scatter(
-            narrow[0].astype(jnp.bfloat16), "fsdp", scatter_dimension=1, tiled=True
-        ).astype(jnp.float32),
-        lax.psum_scatter(
-            narrow[1].astype(jnp.bfloat16), "fsdp", scatter_dimension=1, tiled=True
-        ).astype(jnp.float32),
-        lax.psum_scatter(
-            narrow[2].astype(jnp.bfloat16), "fsdp", scatter_dimension=1, tiled=True
-        ).astype(jnp.float32),
-        lax.psum_scatter(
-            narrow[3].astype(jnp.bfloat16), "fsdp", scatter_dimension=1, tiled=True
-        ).astype(jnp.float32),
-        lax.psum_scatter(
-            narrow[4].astype(jnp.bfloat16), "fsdp", scatter_dimension=1, tiled=True
-        ).astype(jnp.float32),
-        lax.psum_scatter(
-            narrow[5].astype(jnp.bfloat16), "fsdp", scatter_dimension=1, tiled=True
-        ).astype(jnp.float32),
-        lax.psum_scatter(
-            narrow[6].astype(jnp.bfloat16), "fsdp", scatter_dimension=1, tiled=True
-        ).astype(jnp.float32),
-        lax.psum_scatter(
-            narrow[7].astype(jnp.bfloat16), "fsdp", scatter_dimension=1, tiled=True
-        ).astype(jnp.float32),
-        lax.psum_scatter(
-            narrow[8].astype(jnp.bfloat16), "fsdp", scatter_dimension=1, tiled=True
-        ).astype(jnp.float32),
-        lax.psum_scatter(
-            narrow[9].astype(jnp.bfloat16), "fsdp", scatter_dimension=1, tiled=True
-        ).astype(jnp.float32),
-        lax.psum_scatter(
-            narrow[10].astype(jnp.bfloat16), "fsdp", scatter_dimension=1, tiled=True
-        ).astype(jnp.float32),
-        lax.psum_scatter(
-            narrow[11].astype(jnp.bfloat16), "fsdp", scatter_dimension=1, tiled=True
-        ).astype(jnp.float32),
-    )
+PARTS = (0, 1, 2, 0, 1, 2, 2, 0, 2, 1, 0, 1)
+
+
+def mesh_bits():
+    return bits_of(lax.axis_size("dp")), bits_of(lax.axis_size("fsdp"))
+
+
+def gather_weights(shards, norm_params):
+    nd, nf = mesh_bits()
+    devices = 1 << (nd + nf)
+    wide = norm_params.shape[1]
+    padded = jnp.pad(norm_params, ((0, 8 - norm_params.shape[0]), (0, 128 - wide)))
+    blocks = gather_blocks(list(shards) + [padded], PARTS + (0,), nd, nf, 0)
+    weights = []
+    for shard, block in zip(shards, blocks):
+        rows, cols = shard.shape
+        block = block.reshape(1 << nf, rows << nd, cols)
+        weights.append(jnp.swapaxes(block, 0, 1).reshape(rows << nd, cols << nf))
+    norms = blocks[-1].reshape(1 << nf, 1 << nd, 8, 128)[:, :, :4, :wide]
+    norms = norms.transpose(2, 1, 0, 3).reshape(4, devices * wide)
+    return tuple(weights), norms
+
+
+def reduce_grads(grads, norm_rows):
+    nd, nf = mesh_bits()
+    lead = (2,) * (nd + nf)
+    blocks = []
+    for grad in grads:
+        rows, cols = grad.shape[0] >> nd, grad.shape[1] >> nf
+        low = grad.astype(jnp.bfloat16).reshape(grad.shape[0], 1 << nf, cols)
+        blocks.append(jnp.swapaxes(low, 0, 1).reshape(lead + (rows, cols)))
+    wide = norm_rows.shape[1] >> (nd + nf)
+    split = norm_rows.reshape(4, 1 << nd, 1 << nf, wide).transpose(2, 1, 0, 3)
+    split = jnp.pad(split, ((0, 0), (0, 0), (0, 4), (0, 128 - wide)))
+    blocks.append(split.reshape(lead + (8, 128)))
+    owned = reduce_blocks(blocks, PARTS + (0,), nd, nf, 1)
+    return tuple(owned[:-1]), owned[-1][:4, :wide]
 
 
 def stream_forward(resid, context, w_out, w_inner, w_outer, norms, keep):
@@ -226,8 +386,7 @@
         text_inner,
         text_outer,
     )
-    weights = gather_weights(shards)
-    norms = lax.all_gather(norm_params, ("dp", "fsdp"), axis=1, tiled=True)
+    weights, norms = gather_weights(shards, norm_params)
     width_text = text_states.shape[2]
     images = image_states.shape[0]
     length = text_states.shape[1]
@@ -295,21 +454,6 @@
         norms[:, width_text:],
         region_keep,
     )
-    weights = gather_weights(shards)
-    (
-        query_image,
-        key_image,
-        value_image,
-        query_text,
-        key_text,
-        value_text,
-        out_image,
-        out_text,
-        inner_image,
-        outer_image,
-        inner_text,
-        outer_text,
-    ) = weights
     text_dz, text_dcontext, text_wgrads, text_ngrads = stream_backward(
         cot_text.astype(jnp.float32), text_kept, text_context, out_text, inner_text, outer_text
     )
@@ -385,7 +529,6 @@
         text_wgrads[1],
         text_wgrads[2],
     )
-    owned = reduce_grads(local_grads)
     norm_rows = jnp.stack(
         [
             jnp.concatenate([text_ngrads[0], image_ngrads[0]]),
@@ -394,7 +537,7 @@
             jnp.concatenate([text_ngrads[3], image_ngrads[3]]),
         ]
     )
-    norm_grad = lax.psum_scatter(norm_rows, ("dp", "fsdp"), scatter_dimension=1, tiled=True)
+    owned, norm_grad = reduce_grads(local_grads, norm_rows)
     return (
         text_result.astype(jnp.bfloat16),
         image_result.astype(jnp.bfloat16),

time: 1510 us -> 755 us (0.50)
  waiting for transfers between devices: 963 us -> 0 us
  Pallas kernels: 0 us -> 278 us
  blocking collectives: 174 us -> 0 us
  local copies, waits for them, and re-layouts: 61.7 us -> 218 us
  other arithmetic: 69.8 us -> 50.1 us
  matrix products: 217 us -> 201 us
    reduce_scatter x19 -> x0, waiting for transfers between devices: 537 us -> none  [the longest x1 76.3 us: reduce_grads(): lax.psum_scatter(grads[11].astype(jnp.bfloat16), 'dp', scatter_dimension=...]
    pallas_call x0 -> x2, Pallas kernels: none -> 278 us  [the longest x1 144 us: gather_blocks(): pl.pallas_call(functools.partial(gather_kernel, nd, nf, routes), out_shap...]
    all_gather x12 -> x0, waiting for transfers between devices: 229 us -> none  [the longest x1 54.5 us: gather_weights(): lax.all_gather(wider[10], 'dp', axis=0, tiled=True)]
    unnamed x41 -> x0, waiting for transfers between devices: 196 us -> none
    all_gather x13 -> x0, blocking collectives: 134 us -> none  [the longest x1 65.2 us: body(): norms = lax.all_gather(norm_params, ('dp', 'fsdp'), axis=1, tiled=True)]
    reshape x0 -> x28, local copies, waits for them, and re-layouts: none -> 98.8 us  [the longest x15 56.4 us: gather_weights(): weights.append(jnp.swapaxes(block, 0, 1).reshape(rows << nd, cols << nf))]
    transpose x0 -> x12, local copies, waits for them, and re-layouts: none -> 83.5 us  [gather_weights(): weights.append(jnp.swapaxes(block, 0, 1).reshape(rows << nd, cols << nf))]
    unnamed x1 -> x0, blocking collectives: 40.2 us -> none
  transfers between devices with their start and end apart: 36 -> 0, of which waited for: 26 -> 0; matrix products, arithmetic and copies ran while one was open for 22% -> 0% of each run, Pallas kernels for 0% -> 0%
where the time goes in v1:
time: 755 us; the launch traced here: 749 us
  Pallas kernels  278 us (37%)
  local copies, waits for them, and re-layouts  218 us (29%)
  matrix products  201 us (27%)
  other arithmetic  50.1 us (7%)
    pallas_call x1, Pallas kernels, gather_blocks(): pl.pallas_call(functools.partial(gather_kernel, nd, nf, routes), out_shap...  144 us
    pallas_call x1, Pallas kernels, reduce_blocks(): pl.pallas_call(functools.partial(reduce_kernel, nd, nf, routes), out_shap...  134 us
    transpose x12, local copies, waits for them, and re-layouts, gather_weights(): weights.append(jnp.swapaxes(block, 0, 1).reshape(rows << nd, cols << nf))  83.5 us
    dot_general x12, matrix products, project_back(): jnp.einsum('bto,io->bti', grads, matrix, preferred_element_type=jnp.float32)  65.1 us
    reshape x15, local copies, waits for them, and re-layouts, gather_weights(): weights.append(jnp.swapaxes(block, 0, 1).reshape(rows << nd, cols << nf))  56.4 us
    dot_general x12, matrix products, weight_grad(): jnp.einsum('bti,bto->io', inputs, grads, preferred_element_type=jnp.float32)  51.3 us
    dot_general x12, matrix products, project(): jnp.einsum('bti,io->bto', inputs, matrix, preferred_element_type=jnp.floa...  49.3 us
    reshape x12, local copies, waits for them, and re-layouts, reduce_grads(): low = grad.astype(jnp.bfloat16).reshape(grad.shape[0], 1 << nf, cols)  42.3 us

profile of v1, /device:TPU:0, one launch (start us, length us, event | category | flops | bytes accessed | tf_op | source)
XLA Modules:
  0.0 749.3 jit_solution(14781367625660569105)
XLA Ops:
  2.0 144.2 %shard_map.323 = (bf16[2,2,2,2,2,64,512]{6,5,4,3,2,1,0:T(8,128)(2,1)}, bf16[2,2,2,2,2,64,512]{6,5,4,3,2,1,0:T(8,128)(2,1)}, bf16[2,2,2,2,2,64,512]{6,5,4,3,2,1,0...) custom-call(bf16[64,512]{1,0:T(8,128)(2,1)} %refs_0_.1, ...), custom_call_target="tpu_custom_call" | custom-call | tf_op jit(solution)/shard_map/pallas_call | solution.py:120
  146.2 3.7 copy.94
  175.4 3.0 copy.101
  180.6 4.5 fusion.91
  186.3 9.4 %copy.104 = bf16[768,2,1536]{2,1,0:T(2,128)(2,1)} copy(bf16[768,2,1536]{2,0,1:T(8,128)(2,1)} %bitcast.290) | data formatting | bytes 9437184 | tf_op jit(solution)/shard_map/transpose | solution.py:294
  195.6 11.9 %reshape.540 = bf16[768,3072,1]{1,0,2:T(8,128)(2,1)} reshape(bf16[768,2,1536]{2,1,0:T(2,128)(2,1)} %copy.104) | data formatting | bytes 9437184 | tf_op jit(solution)/shard_map/reshape | solution.py:294
  207.6 10.4 %fusion.11 = (u8[128,3072]{1,0:T(8,128)(4,1)S(1)}, u8[128,3072]{1,0:T(8,128)(4,1)S(1)}, f32[8,128,3072]{2,1,0:T(8,128)S(1)}) fusion(bf16[768,3072,1]{1,0,2:T(8,128)(2,1)} %reshape.540, f32[8,128,768]{2,1,0:T(8,128)S(1)} %get-tuple-element.154, f32[768]{0:T(1024)S(1)} %get-tuple-element.125, f32[768]{0:T(1024)S(1)} %get-tuple-element.126, ...), kind=kOutput, calls=%fused_computation.56 | convolution fusion | flops 4875878400 | bytes 21248000 | tf_op jit(solution)/shard_map/bti,io->bto/dot_general | solution.py:258
  218.0 29.2 %multiply_convert_fusion = (bf16[8,128,3072]{2,1,0:T(8,128)(2,1)}, f32[8,128,3072]{2,1,0:T(8,128)}) fusion(f32[8,128,3072]{2,1,0:T(8,128)S(1)} %get-tuple-element.155, u8[128,3072]{1,0:T(8,128)(4,1)S(1)} %get-tuple-element.104, u8[128,3072]{1,0:T(8,128)(4,1)S(1)} %get-tuple-element.103), kind=kLoop, calls=%fused_computation.12 | loop fusion | flops 220200960 | bytes 32243712 | tf_op jit(solution)/shard_map/convert_element_type | solution.py:321
  247.2 44.9 %copy.105 = bf16[3072,2,384]{2,1,0:T(2,128)(2,1)} copy(bf16[3072,2,384]{2,0,1:T(8,128)(2,1)S(1)} %bitcast.289) | data formatting | bytes 9437184 | tf_op jit(solution)/shard_map/transpose | solution.py:294
  292.1 11.4 %reshape.541 = bf16[3072,768,1]{1,0,2:T(8,128)(2,1)} reshape(bf16[3072,2,384]{2,1,0:T(2,128)(2,1)} %copy.105) | data formatting | bytes 9437184 | tf_op jit(solution)/shard_map/reshape | solution.py:294
  303.5 9.0 %fusion.92 = (f32[8,128]{1,0:T(8,128)S(1)}, f32[8,128,768]{2,1,0:T(8,128)S(1)}) fusion(bf16[8,128,3072]{2,1,0:T(8,128)(2,1)} %get-tuple-element.133, bf16[3072,768,1]{1,0,2:T(8,128)(2,1)} %reshape.541, f32[768]{0:T(1024)S(1)} %get-tuple-element.125, f32[768]{0:T(1024)S(1)} %get-tuple-element.126, f32[8,128]{1,0:T(8,128)S(1)} %fusion.75, ...), kind=kOutput, calls=%fused_computation.220 | convolution fusion | flops 4836555776 | bytes 17319936 | tf_op jit(solution)/shard_map/bti,io->bto/dot_general | solution.py:258
  314.1 3.1 multiply_reduce_fusion
  317.3 17.4 %add_convert_fusion = bf16[8,128,3072]{2,1,0:T(8,128)(2,1)} fusion(f32[8,128,3072]{2,1,0:T(8,128)} %get-tuple-element.134, f32[8,128,3072]{2,1,0:T(8,128)} %copy-done.2, bf16[3072,768,1]{1,0,2:T(8,128)(2,1)} %reshape.541, f32[8,128]{1,0:T(8,128)S(1)} %negate_multiply_fusion.5, bf16[8,128,768]{2,1,0:T(8,128)(2,1)} %param.38, f32[8,128,768]{2,1,0:T(8,128)} %copy-done.3, ...), kind=kOutput, calls=%fused_computation.11 | convolution fusion | flops 4883742720 | bytes 40918016 | tf_op jit(solution)/shard_map/bto,io->bti/dot_general | solution.py:262
  334.7 12.1 %multiply_reduce_fusion.1 = (f32[768]{0:T(1024)S(1)}, f32[8,128]{1,0:T(8,128)S(1)}, f32[768]{0:T(1024)S(1)}, f32[8,128,768]{2,1,0:T(8,128)}) fusion(f32[8,128,768]{2,1,0:T(8,128)S(1)} %get-tuple-element.154, f32[8,128]{1,0:T(8,128)S(1)} %fusion.75, f32[8,128]{1,0:T(8,128)S(1)} %broadcast_multiply_fusion.3, f32[768]{0:T(1024)S(1)} %get-tuple-element.126, ...), kind=kOutput, calls=%fused_computation.43 | convolution fusion | flops 4845990912 | bytes 22065152 | tf_op jit(solution)/shard_map/bto,io->bti/dot_general | solution.py:262
  346.8 3.5 copy.108
  350.3 4.4 reshape.543
  354.7 3.8 convolution_convert_fusion.7
  368.1 3.1 convolution_convert_fusion.3
  371.3 7.8 %fusion.42 = bf16[8,36,8,128]{3,1,2,0:T(8,128)(2,1)} fusion(bf16[8,128,8,128]{1,3,2,0:T(8,128)(2,1)} %bitcast.336, f32[8,8,36]{2,1,0:T(8,128)S(1)} %get-tuple-element.158, f32[8,8,36,128]{3,2,1,0:T(8,128)} %copy-done.23), kind=kOutput, calls=%fused_computation.139 | convolution fusion | flops 76679552 | bytes 3875840 | tf_op jit(solution)/shard_map/bhrl,blhe->brhe/dot_general | solution.py:428
  383.2 5.1 copy.116
  388.2 4.5 reshape.545
  392.7 3.4 fusion.94
  397.6 3.4 copy.118
  401.1 4.4 reshape.546
  405.5 3.4 fusion.67
  410.0 4.0 multiply_convert_fusion.7
  414.0 3.5 copy.119
  417.5 4.8 reshape.547
  422.3 3.3 fusion.95
  434.7 12.2 %bitcast_convert_fusion = bf16[3072,768]{0,1:T(8,128)(2,1)} fusion(bf16[8,128,3072]{2,1,0:T(8,128)(2,1)} %get-tuple-element.133, f32[8,128]{1,0:T(8,128)S(1)} %negate_multiply_fusion.5, bf16[8,128,768]{2,1,0:T(8,128)(2,1)} %param.38, f32[8,128,768]{2,1,0:T(8,128)} %copy-done.3, f32[8,128]{1,0:T(8,128)S(1)} %get-tuple-element.145, ...), kind=kOutput, calls=%fused_computation.25 | convolution fusion | flops 4842061824 | bytes 15752192 | tf_op jit(solution)/shard_map/bti,bto->io/dot_general | solution.py:266
  446.9 6.6 copy.158
  453.6 8.5 %bitcast_convert_fusion.1 = bf16[768,3072]{1,0:T(8,128)(2,1)S(1)} fusion(bf16[8,128,3072]{2,1,0:T(8,128)(2,1)} %add_convert_fusion, f32[8,128,768]{2,1,0:T(8,128)S(1)} %get-tuple-element.154, f32[768]{0:T(1024)S(1)} %get-tuple-element.125, f32[768]{0:T(1024)S(1)} %get-tuple-element.126, f32[8,128]{1,0:T(8,128)S(1)} %fusion.75, ...), kind=kOutput, calls=%fused_computation.26 | convolution fusion | flops 4838129664 | bytes 14170112 | tf_op jit(solution)/shard_map/bti,bto->io/dot_general | solution.py:266
  464.7 3.3 bitcast_convert_fusion.2
  468.0 4.0 copy.154
  472.0 4.2 bitcast_convert_fusion.3
  476.2 3.9 copy.153
  492.5 4.1 copy.149
  496.6 5.1 convert_bitcast_fusion
  508.7 4.1 copy.144
  512.8 3.1 multiply_reduce_fusion.11
  522.4 4.3 copy.142
  539.1 4.0 copy.140
  543.1 8.3 %convolution_convert_fusion = bf16[8,8,128,128]{3,2,1,0:T(8,128)(2,1)} fusion(bf16[8,36,8,128]{3,2,1,0:T(8,128)(2,1)S(1)} %copy-done.68, f32[8,8,36]{2,1,0:T(8,128)S(1)} %get-tuple-element.158, f32[8,8,36,128]{3,2,1,0:T(8,128)} %copy-done.23), kind=kOutput, calls=%fused_computation.70 | convolution fusion | flops 77433216 | bytes 3875840 | tf_op jit(solution)/shard_map/bhrl,brhe->blhe/dot_general | solution.py:473
  551.4 5.0 bitcast_convert_fusion.9
  570.9 133.5 %shard_map.324 = (f32[64,512]{1,0:T(8,128)}, f32[64,512]{1,0:T(8,128)}, f32[64,512]{1,0:T(8,128)}, f32[48,512]{1,0:T(8,128)}, f32[48,512]{1,0:T(8,128)}, /*index...) custom-call(bf16[2,2,2,2,2,64,512]{6,5,4,3,2,1,0:T(8,128)(2,1)} %bit, ...), custom_call_target="tpu_custom_call" | custom-call | tf_op jit(solution)/shard_map/pallas_call | solution.py:227
  715.5 5.2 fusion.96
  723.4 5.2 fusion.97
  731.5 8.4 %add_add_fusion.2 = f32[8,128,768]{2,1,0:T(8,128)} fusion(f32[8,128,768]{2,1,0:T(8,128)} %fusion.97, f32[8,128,768]{2,1,0:T(8,128)} %fusion.96, f32[8,128,768]{2,1,0:T(8,128)} %copy-done.32, bf16[8,128,1024]{1,2,0:T(8,128)(2,1)} %bitcast.339, bf16[768,1024,1]{1,0,2:T(8,128)(2,1)S(1)} %reshape.550, f32[8,128]{1,0:T(8,128)S(1)} %negate_multiply_fusion.4), kind=kOutput, calls=%fused_computation.44 | convolution fusion | flops 1613758464 | bytes 16257024 | tf_op jit(solution)/shard_map/bto,io->bti/dot_general | solution.py:262
  (312 shorter events, 137.4 us)
Async XLA Ops:
  0.7 152.8 %copy-start = (bf16[2,36,1024]{2,0,1:T(2,128)(2,1)S(1)}, bf16[2,36,1024]{2,0,1:T(2,128)(2,1)}, u32[]{:S(2)}) copy-start(bf16[2,36,1024]{2,0,1:T(2,128)(2,1)} %param.21) | copy-start | bytes 442372
  149.9 2.9 copy-start.91
  152.9 4.9 copy-start.88
  157.2 4.4 copy-start.17
  157.9 272.5 %copy-start.83 = (f32[8,36]{1,0:T(8,128)}, f32[8,36]{1,0:T(8,128)S(1)}, u32[]{:S(2)}) copy-start(f32[8,36]{1,0:T(8,128)S(1)} %get-tuple-element.136) | copy-start | bytes 3460
  162.4 10.7 %copy-start.22 = (f32[8,8,36,128]{3,2,1,0:T(8,128)}, f32[8,8,36,128]{3,2,1,0:T(8,128)S(1)}, u32[]{:S(2)}) copy-start(f32[8,8,36,128]{3,2,1,0:T(8,128)S(1)} %fusion.27) | copy-start | bytes 3538948
  163.7 9.4 %copy-start.71 = (f32[8,8,128]{2,1,0:T(8,128)}, f32[8,8,128]{2,1,0:T(8,128)S(1)}, u32[]{:S(2)}) copy-start(f32[8,8,128]{2,1,0:T(8,128)S(1)} %get-tuple-element.151) | copy-start | bytes 98308
  218.0 29.2 %copy-start.2 = (f32[8,128,3072]{2,1,0:T(8,128)}, f32[8,128,3072]{2,1,0:T(8,128)S(1)}, u32[]{:S(2)}) copy-start(f32[8,128,3072]{2,1,0:T(8,128)S(1)} %get-tuple-element.155) | copy-start | bytes 37748740
  218.0 29.2 %slice-start = ((s8[4718592]{0:T(1024)(128)(4,1)}), s8[4194304]{0:T(1024)(128)(4,1)S(1)}, s32[]{:S(2)}) async-start(s8[4718592]{0:T(1024)(128)(4,1)} %bitcast.287), calls=%async_computation | async-start | bytes 8388608
  218.0 29.2 %slice-start.1 = ((s8[4718592]{0:T(1024)(128)(4,1)}), s8[524288]{0:T(1024)(128)(4,1)S(1)}, s32[]{:S(2)}) async-start(s8[4718592]{0:T(1024)(128)(4,1)} %bitcast.287), calls=%async_computation.1 | async-start | bytes 1048576
  303.5 9.0 %copy-start.92 = (s32[8]{0:T(128)S(1)}, s32[8]{0:T(128)}, u32[]{:S(2)}) copy-start(s32[8]{0:T(128)} %param.22) | copy-start | bytes 100
  303.5 9.1 %copy-start.15 = (bf16[8,128,768]{2,1,0:T(8,128)(2,1)S(1)}, bf16[8,128,768]{2,1,0:T(8,128)(2,1)}, u32[]{:S(2)}) copy-start(bf16[8,128,768]{2,1,0:T(8,128)(2,1)} %param.38) | copy-start | bytes 4718596
  334.7 12.1 %copy-start.43 = (bf16[2,2,2,2,2,64,512]{6,5,4,3,2,1,0:T(8,128)(2,1)S(1)}, bf16[2,2,2,2,2,64,512]{6,5,4,3,2,1,0:T(8,128)(2,1)}, u32[]{:S(2)}) copy-start(bf16[2,2,2,2,2,64,512]{6,5,4,3,2,1,0:T(8,128)(2,1)} %get-tuple-element.51) | copy-start | bytes 6291460
  350.2 4.4 copy-start.90
  392.7 4.9 copy-start.42
  408.9 5.0 copy-start.41
  422.3 3.3 copy-start.38
  422.3 6.1 copy-start.56
  425.5 4.9 copy-start.30
  430.5 3.0 copy-start.93
  486.7 3.1 copy-start.66
  492.5 4.1 copy-start.16
  496.6 5.1 copy-start.72
  508.7 4.1 copy-start.21
  508.7 4.1 copy-start.65
  519.5 3.0 copy-start.36
  526.8 3.1 copy-start.24
  536.2 3.0 copy-start.62
  539.1 4.0 copy-start.68
  559.9 3.4 copy-start.48
  570.9 134.8 %copy-start.29 = (f32[8,36,1024]{2,1,0:T(8,128)S(1)}, f32[8,36,1024]{2,1,0:T(8,128)}, u32[]{:S(2)}) copy-start(f32[8,36,1024]{2,1,0:T(8,128)} %copy-done.28) | copy-start | bytes 3538948
  570.9 134.8 %copy-start.40 = (bf16[1024,1024,1]{1,0,2:T(8,128)(2,1)S(1)}, bf16[1024,1024,1]{1,0,2:T(8,128)(2,1)}, u32[]{:S(2)}) copy-start(bf16[1024,1024,1]{1,0,2:T(8,128)(2,1)} %reshape.543) | copy-start | bytes 6291460
  715.5 5.2 copy-start.13
  723.4 5.2 copy-start.12
  731.4 8.5 %copy-start.33 = (bf16[8,36,1024]{2,1,0:T(8,128)(2,1)S(1)}, bf16[8,36,1024]{2,1,0:T(8,128)(2,1)}, u32[]{:S(2)}) copy-start(bf16[8,36,1024]{2,1,0:T(8,128)(2,1)} %get-tuple-element.140) | copy-start | bytes 1769476
  731.4 9.6 %copy-start.78 = (f32[64,512]{1,0:T(8,128)S(1)}, f32[64,512]{1,0:T(8,128)}, u32[]{:S(2)}) copy-start(f32[64,512]{1,0:T(8,128)} %get-tuple-element.196) | copy-start | bytes 393220
  731.4 10.3 %copy-start.77 = (f32[64,512]{1,0:T(8,128)S(1)}, f32[64,512]{1,0:T(8,128)}, u32[]{:S(2)}) copy-start(f32[64,512]{1,0:T(8,128)} %get-tuple-element.197) | copy-start | bytes 393220
  731.5 10.9 %copy-start.76 = (f32[64,512]{1,0:T(8,128)S(1)}, f32[64,512]{1,0:T(8,128)}, u32[]{:S(2)}) copy-start(f32[64,512]{1,0:T(8,128)} %get-tuple-element.198) | copy-start | bytes 393220
  739.8 3.2 copy-start.82
  739.8 3.8 copy-start.81
  739.8 4.5 copy-start.80
  739.9 5.1 copy-start.75
  739.9 5.8 copy-start.79
  739.9 6.4 copy-start.74
  739.9 7.1 copy-start.73
  739.9 7.7 %copy-start.70 = (f32[48,1536]{1,0:T(8,128)S(1)}, f32[48,1536]{1,0:T(8,128)}, u32[]{:S(2)}) copy-start(f32[48,1536]{1,0:T(8,128)} %get-tuple-element.206) | copy-start | bytes 884740
  739.9 9.1 %copy-start.1 = (bf16[2,36,1024]{2,0,1:T(2,128)(2,1)S(1)}, bf16[2,36,1024]{2,0,1:T(2,128)(2,1)}, u32[]{:S(2)}) copy-start(bf16[2,36,1024]{2,0,1:T(2,128)(2,1)} %param.21) | copy-start | bytes 442372
  739.9 8.4 %copy-start.69 = (f32[192,384]{1,0:T(8,128)S(1)}, f32[192,384]{1,0:T(8,128)}, u32[]{:S(2)}) copy-start(f32[192,384]{1,0:T(8,128)} %get-tuple-element.207) | copy-start | bytes 884740
  (48 other events, 96.8 us)

commit v2 on v1

v2 whole, which is shorter than its diff:
```python
import functools
import math

import jax
import jax.numpy as jnp
from jax import lax
from jax.experimental import pallas as pl
from jax.experimental.pallas import tpu as pltpu
from jax.sharding import PartitionSpec as P

HDIM = 128

norm_eps = 1e-12
masked_score = -1e30

MESH_IDS = pl.DeviceIdType.MESH


def bits_of(size):
    count = size.bit_length() - 1
    assert 1 << count == size
    return count


def hop_orders(nd, nf):
    high = [("d", b) for b in range(nd - 1, 2, -1)]
    low = [("d", 2)]
    near = [("d", 1)]
    wide = [("f", b) for b in range(nf)]
    return (
        high + near + low + wide,
        low + high + wide + near,
        high + wide + near + low,
    )


CORE = ("d", 0)


class Place:
    def __init__(self, nd, nf):
        self.d = lax.axis_index("dp")
        self.f = lax.axis_index("fsdp")
        self.axes = [("f", b) for b in range(nf - 1, -1, -1)] + [
            ("d", b) for b in range(nd - 1, -1, -1)
        ]

    def bit(self, axis):
        value = self.f if axis[0] == "f" else self.d
        return lax.rem(value // (1 << axis[1]), 2)

    def partner(self, axis):
        step = (1 << axis[1]) * (1 - 2 * self.bit(axis))
        if axis[0] == "f":
            return (self.d, self.f + step)
        return (self.d + step, self.f)

    def index(self, whole, flip=None):
        picked = []
        for axis in self.axes:
            if axis in whole:
                picked.append(slice(None))
            elif axis == flip:
                picked.append(1 - self.bit(axis))
            else:
                picked.append(self.bit(axis))
        return tuple(picked)

    def barrier(self):
        sem = pltpu.get_barrier_semaphore()
        for axis in self.axes:
            pl.semaphore_signal(
                sem, inc=1, device_id=self.partner(axis), device_id_type=MESH_IDS
            )
        pl.semaphore_wait(sem, len(self.axes))


def gather_kernel(nd, nf, routes, *refs):
    count = len(routes)
    ins, outs = refs[:count], refs[count : 2 * count]
    local_sem, send_sem, recv_sem = refs[2 * count :]
    place = Place(nd, nf)
    local = []
    for m in range(count):
        copy = pltpu.make_async_copy(ins[m], outs[m].at[place.index(())], local_sem.at[m])
        copy.start()
        local.append(copy)
    place.barrier()
    hops = len(routes[0])
    sent = [[] for _ in range(count)]
    for h in range(hops):
        for m in range(count):
            if h == 0:
                local[m].wait()
            else:
                sent[m][h - 1].wait_recv()
            region = outs[m].at[place.index(routes[m][:h])]
            copy = pltpu.make_async_remote_copy(
                src_ref=region,
                dst_ref=region,
                send_sem=send_sem.at[m, h],
                recv_sem=recv_sem.at[m, h],
                device_id=place.partner(routes[m][h]),
                device_id_type=MESH_IDS,
            )
            copy.start()
            sent[m].append(copy)
    for m in range(count):
        sent[m][hops - 1].wait_recv()
        for h in range(hops):
            sent[m][h].wait_send()


def gather_blocks(shards, parts, nd, nf, collective_id):
    orders = hop_orders(nd, nf)
    routes = [tuple(orders[part]) + (CORE,) for part in parts]
    count, hops = len(shards), len(routes[0])
    lead = (2,) * (nd + nf)
    return pl.pallas_call(
        functools.partial(gather_kernel, nd, nf, routes),
        out_shape=[jax.ShapeDtypeStruct(lead + s.shape, s.dtype) for s in shards],
        in_specs=[pl.BlockSpec(memory_space=pl.ANY)] * count,
        out_specs=[pl.BlockSpec(memory_space=pl.ANY)] * count,
        scratch_shapes=[
            pltpu.SemaphoreType.DMA((count,)),
            pltpu.SemaphoreType.DMA((count, hops)),
            pltpu.SemaphoreType.DMA((count, hops)),
        ],
        compiler_params=pltpu.CompilerParams(
            collective_id=collective_id, has_side_effects=True
        ),
    )(*shards)


def add_blocks(place, acc, index, incoming, out=None):
    lead = incoming.shape[:-2]
    total = math.prod(lead)

    def spot(i):
        inner = []
        for size in reversed(lead):
            inner.append(lax.rem(i, size))
            i = i // size
        return tuple(reversed(inner))

    def full(at):
        at = list(at)
        return tuple(at.pop(0) if isinstance(p, slice) else p for p in index)

    if out is not None:
        out[...] = acc[index].astype(jnp.float32) + incoming[...].astype(jnp.float32)
        return

    def one(i, carry):
        at = spot(i)
        where = full(at)
        acc[where] = acc[where] + incoming[at]
        return carry

    lax.fori_loop(0, total, one, 0)


def reduce_kernel(nd, nf, routes, *refs):
    count = len(routes)
    hops = len(routes[0])
    ins, outs = refs[:count], refs[count : 2 * count]
    accs = refs[2 * count : 3 * count]
    temps = [refs[3 * count + m * hops : 3 * count + (m + 1) * hops] for m in range(count)]
    local_sem, send_sem, recv_sem = refs[3 * count + count * hops :]
    place = Place(nd, nf)
    rest = [axis for axis in place.axes if axis != CORE]
    local = []
    for m in range(count):
        copy = pltpu.make_async_copy(ins[m].at[place.index(rest)], accs[m], local_sem.at[m])
        copy.start()
        local.append(copy)
    place.barrier()
    sent = [[] for _ in range(count)]

    def send(m, h, region):
        copy = pltpu.make_async_remote_copy(
            src_ref=region,
            dst_ref=temps[m][h],
            send_sem=send_sem.at[m, h],
            recv_sem=recv_sem.at[m, h],
            device_id=place.partner(routes[m][h]),
            device_id_type=MESH_IDS,
        )
        copy.start()
        sent[m].append(copy)

    def within(m, h, flip=None):
        whole = routes[m][h + 1 :]
        full = place.index(whole, flip)
        return tuple(p for p, axis in zip(full, place.axes) if axis != CORE)

    for m in range(count):
        send(m, 0, ins[m].at[place.index(routes[m][1:], CORE)])
    for m in range(count):
        local[m].wait()
    for h in range(1, hops + 1):
        for m in range(count):
            sent[m][h - 1].wait_recv()
            here = within(m, h - 1)
            if h == hops:
                add_blocks(place, accs[m], here, temps[m][h - 1], outs[m])
            else:
                add_blocks(place, accs[m], here, temps[m][h - 1])
                send(m, h, accs[m].at[within(m, h, routes[m][h])])
    for m in range(count):
        for h in range(hops):
            sent[m][h].wait_send()


def reduce_blocks(blocks, parts, nd, nf, collective_id):
    orders = hop_orders(nd, nf)
    routes = [(CORE,) + tuple(reversed(orders[part])) for part in parts]
    count, hops = len(blocks), len(routes[0])
    shapes = [b.shape[-2:] for b in blocks]
    scratch = [
        pltpu.VMEM((2,) * (nd + nf - 1) + s, b.dtype) for s, b in zip(shapes, blocks)
    ]
    for s, b in zip(shapes, blocks):
        for h in range(hops):
            scratch.append(pltpu.VMEM((2,) * (hops - 1 - h) + s, b.dtype))
    return pl.pallas_call(
        functools.partial(reduce_kernel, nd, nf, routes),
        out_shape=[jax.ShapeDtypeStruct(s, jnp.float32) for s in shapes],
        in_specs=[pl.BlockSpec(memory_space=pl.ANY)] * count,
        out_specs=[pl.BlockSpec(memory_space=pltpu.VMEM)] * count,
        scratch_shapes=scratch
        + [
            pltpu.SemaphoreType.DMA((count,)),
            pltpu.SemaphoreType.DMA((count, hops)),
            pltpu.SemaphoreType.DMA((count, hops)),
        ],
        compiler_params=pltpu.CompilerParams(
            collective_id=collective_id,
            has_side_effects=True,
            vmem_limit_bytes=60 * 1024 * 1024,
        ),
    )(*blocks)


def dot_nn(a, b):
    return lax.dot_general(a, b, (((1,), (0,)), ((), ())), preferred_element_type=jnp.float32)


def dot_nt(a, b):
    return lax.dot_general(a, b, (((1,), (1,)), ((), ())), preferred_element_type=jnp.float32)


def dot_tn(a, b):
    return lax.dot_general(a, b, (((0,), (0,)), ((), ())), preferred_element_type=jnp.float32)


def low(value):
    return value.astype(jnp.bfloat16)


def times(value, matrix):
    parts = [dot_nn(value, matrix[f]) for f in range(matrix.shape[0])]
    return parts[0] if len(parts) == 1 else jnp.concatenate(parts, axis=1)


def times_back(value, matrix):
    cols = matrix.shape[2]
    total = None
    for f in range(matrix.shape[0]):
        term = dot_nt(value[:, f * cols : (f + 1) * cols], matrix[f])
        total = term if total is None else total + term
    return total


VMEM_LIMIT = 60 * 1024 * 1024
WHOLE = pl.BlockSpec(memory_space=pltpu.VMEM)
SCALARS = pl.BlockSpec(memory_space=pltpu.SMEM)


def project_rows(x_ref, w_ref, out_ref, block):
    cols = w_ref.shape[2]

    def one(i, carry):
        at = pl.ds(pl.multiple_of(i * block, block), block)
        rows = x_ref[at, :]
        for f in range(w_ref.shape[0]):
            out_ref[at, f * cols : (f + 1) * cols] = low(dot_nn(rows, w_ref[f]))
        return carry

    lax.fori_loop(0, x_ref.shape[0] // block, one, 0)


def softmax(scores, axis):
    top = jnp.max(scores, axis=axis, keepdims=True)
    weight = jnp.exp(scores - top)
    return weight / jnp.sum(weight, axis=axis, keepdims=True)


def attention_pair(p, refs):
    (lens, owner, counts, iq, ik, iv, tq, tk, tv, iprob, tprob, ictx, tctx) = refs
    regions = iprob.shape[1]
    length = tq.shape[0] // lens.shape[0]
    heads = tq.shape[1] // HDIM
    scale = 1.0 / math.sqrt(HDIM)
    image = owner[p]
    kept_text = lax.broadcasted_iota(jnp.int32, (regions, length), 1) < lens[p]
    kept_region = lax.broadcasted_iota(jnp.int32, (regions, length), 0) < counts[p]
    rows_t = pl.ds(pl.multiple_of(p * length, length), length)
    rows_i = pl.ds(pl.multiple_of(p * regions, regions), regions)
    for h in range(heads):
        at = slice(h * HDIM, (h + 1) * HDIM)
        scores = scale * dot_nt(iq[image, :, at], tk[rows_t, at])
        probs = softmax(jnp.where(kept_text, scores, masked_score), 1)
        iprob[p * heads + h] = probs
        ictx[rows_i, at] = low(dot_nn(low(probs), tv[rows_t, at]))
        scores = scale * dot_nt(ik[image, :, at], tq[rows_t, at])
        probs = softmax(jnp.where(kept_region, scores, masked_score), 0)
        tprob[p * heads + h] = probs
        tctx[rows_t, at] = low(dot_tn(low(probs), iv[image, :, at]))


def forward_kernel(lens, owner, counts, text, image, *refs):
    weights, (iq, ik, iv, tq, tk, tv, iprob, tprob, ictx, tctx) = refs[:6], refs[6:]
    for w_ref, out_ref in zip(weights[:3], (iq, ik, iv)):
        wide = times(image[...], w_ref)
        out_ref[...] = low(wide).reshape(out_ref.shape)
    for w_ref, out_ref in zip(weights[3:], (tq, tk, tv)):
        project_rows(text, w_ref, out_ref, 256)
    shared = (lens, owner, counts, iq, ik, iv, tq, tk, tv, iprob, tprob, ictx, tctx)

    def one(p, carry):
        attention_pair(p, shared)
        return carry

    lax.fori_loop(0, lens.shape[0], one, 0)


def forward_attention(lens, owner, counts, text, image, weights, images):
    pairs = lens.shape[0]
    regions = image.shape[0] // images
    wide = weights[0].shape[0] * weights[0].shape[2]
    heads = wide // HDIM
    length = text.shape[0] // pairs
    bf = jnp.bfloat16
    shapes = (
        [jax.ShapeDtypeStruct((images, regions, wide), bf)] * 3
        + [jax.ShapeDtypeStruct((text.shape[0], wide), bf)] * 3
        + [jax.ShapeDtypeStruct((pairs * heads, regions, length), jnp.float32)] * 2
        + [
            jax.ShapeDtypeStruct((pairs * regions, wide), bf),
            jax.ShapeDtypeStruct((text.shape[0], wide), bf),
        ]
    )
    return pl.pallas_call(
        forward_kernel,
        out_shape=shapes,
        in_specs=[SCALARS] * 3 + [WHOLE] * 8,
        out_specs=[WHOLE] * len(shapes),
        compiler_params=pltpu.CompilerParams(vmem_limit_bytes=VMEM_LIMIT),
    )(lens, owner, counts, text, image, *weights)


def gelu_pair(x):
    scaled = jnp.abs(x) * (1.0 / math.sqrt(2.0))
    bell = jnp.exp(-0.5 * x * x)
    t = 1.0 / (1.0 + 0.3275911 * scaled)
    poly = t * (
        0.254829592
        + t * (-0.284496736 + t * (1.421413741 + t * (-1.453152027 + t * 1.061405429)))
    )
    tail = 0.5 * poly * bell
    below = jnp.where(x < 0, tail, 1.0 - tail)
    return x * below, below + x * bell * (1.0 / math.sqrt(2.0 * math.pi))


def row_mean(value):
    return jnp.mean(value, axis=-1, keepdims=True)


def col_sum(value):
    return jnp.sum(value, axis=0, keepdims=True)


def stream_kernel(x, ctx, cot, keep, norms, w_out, w_inner, w_outer, *refs):
    (out, dz_out, mid_out, act_out, hid_out, ffn_out, branch_out, dctx_out, ngrad, slope) = refs

    def normalize(z):
        offset = z - row_mean(z)
        inv = lax.rsqrt(row_mean(offset * offset) + norm_eps)
        return offset * inv, inv

    def normalize_back(dy, xhat, inv, gain):
        dx = dy * gain
        return inv * (dx - row_mean(dx) - xhat * row_mean(dx * xhat))

    kept = keep[...]
    first_hat, first_inv = normalize(x[...].astype(jnp.float32) + times(ctx[...], w_out))
    mid = first_hat * norms[0:1, :] + norms[1:2, :]
    mid_low = low(mid)
    mid_out[...] = mid_low
    cols = w_inner.shape[2]
    for f in range(w_inner.shape[0]):
        at = slice(f * cols, (f + 1) * cols)
        act, grad = gelu_pair(dot_nn(mid_low, w_inner[f]))
        act_out[:, at] = low(act)
        slope[:, at] = grad
    second_hat, second_inv = normalize(mid + times(act_out[...], w_outer))
    out[...] = low((second_hat * norms[2:3, :] + norms[3:4, :]) * kept)
    dy = cot[...].astype(jnp.float32) * kept
    second_dz = normalize_back(dy, second_hat, second_inv, norms[2:3, :])
    ffn_low = low(second_dz)
    ffn_out[...] = ffn_low
    rows = [col_sum(dy * second_hat), col_sum(dy)]
    hid_out[...] = low(times_back(ffn_low, w_outer) * slope[...])
    mid_grad = second_dz + times_back(hid_out[...], w_inner)
    first_dz = normalize_back(mid_grad, first_hat, first_inv, norms[0:1, :])
    dz_out[...] = first_dz
    branch_low = low(first_dz)
    branch_out[...] = branch_low
    dctx_out[...] = low(times_back(branch_low, w_out))
    rows = [col_sum(mid_grad * first_hat), col_sum(mid_grad)] + rows

    @pl.when(pl.program_id(0) == 0)
    def _():
        ngrad[...] = jnp.zeros_like(ngrad)

    for r in range(4):
        ngrad[r : r + 1, :] += rows[r]


def stream(x, ctx, cot, keep, norms, w_out, w_inner, w_outer, block):
    rows, wide = x.shape
    inner = w_inner.shape[0] * w_inner.shape[2]
    bi = ctx.shape[1]
    bf, f32 = jnp.bfloat16, jnp.float32

    def by_row(cols):
        return pl.BlockSpec((block, cols), lambda i: (i, 0))

    def resident(shape):
        return pl.BlockSpec(
            shape, lambda i: (0,) * len(shape), pipeline_mode=pl.Buffered(1)
        )

    outs = [
        (wide, bf),
        (wide, f32),
        (wide, bf),
        (inner, bf),
        (inner, bf),
        (wide, bf),
        (wide, bf),
        (bi, bf),
    ]
    return pl.pallas_call(
        stream_kernel,
        grid=(rows // block,),
        in_specs=[by_row(wide), by_row(bi), by_row(wide), by_row(1)]
        + [resident(v.shape) for v in (norms, w_out, w_inner, w_outer)],
        out_specs=[by_row(cols) for cols, _ in outs]
        + [pl.BlockSpec((4, wide), lambda i: (0, 0))],
        out_shape=[jax.ShapeDtypeStruct((rows, cols), dt) for cols, dt in outs]
        + [jax.ShapeDtypeStruct((4, wide), f32)],
        scratch_shapes=[pltpu.VMEM((block, inner), f32)],
        compiler_params=pltpu.CompilerParams(vmem_limit_bytes=VMEM_LIMIT),
    )(x, ctx, cot, keep, norms, w_out, w_inner, w_outer)


def weight_grad_kernel(x, d, out):
    out[0] = low(dot_tn(x[...], d[...]))


def weight_grad(x, d, splits):
    rows, inner = x.shape
    cols = d.shape[1] // splits
    block = 512 if inner % 512 == 0 else 256
    return pl.pallas_call(
        weight_grad_kernel,
        grid=(splits, inner // block),
        in_specs=[
            pl.BlockSpec((rows, block), lambda f, i: (0, i)),
            pl.BlockSpec((rows, cols), lambda f, i: (0, f)),
        ],
        out_specs=pl.BlockSpec((1, block, cols), lambda f, i: (f, i, 0)),
        out_shape=jax.ShapeDtypeStruct((splits, inner, cols), jnp.bfloat16),
        compiler_params=pltpu.CompilerParams(vmem_limit_bytes=VMEM_LIMIT),
    )(x, d)


def attention_back_pair(p, refs):
    (owner, iq, ik, iv, tq, tk, tv, iprob, tprob, dic, dtc, diq, dik, div, dtq, dtk, dtv) = refs
    regions = iprob.shape[1]
    length = tq.shape[0] // owner.shape[0]
    heads = tq.shape[1] // HDIM
    scale = 1.0 / math.sqrt(HDIM)
    image = owner[p]
    rows_t = pl.ds(pl.multiple_of(p * length, length), length)
    rows_i = pl.ds(pl.multiple_of(p * regions, regions), regions)

    def add_to(ref, at, value):
        value = low(value).astype(jnp.float32)
        for i in range(ref.shape[0]):
            ref[i, :, at] += jnp.where(image == i, value, 0.0)

    for h in range(heads):
        at = slice(h * HDIM, (h + 1) * HDIM)
        grad = dic[rows_i, at]
        probs = iprob[p * heads + h]
        keys = tk[rows_t, at]
        dprobs = dot_nt(grad, tv[rows_t, at])
        dtv[rows_t, at] = low(dot_tn(low(probs), grad))
        inner = jnp.sum(probs * dprobs, axis=1, keepdims=True)
        dscores = low(probs * (dprobs - inner))
        add_to(diq, at, scale * dot_nn(dscores, keys))
        dtk[rows_t, at] = low(scale * dot_tn(dscores, iq[image, :, at]))
        grad = dtc[rows_t, at]
        probs = tprob[p * heads + h]
        dprobs = dot_nt(iv[image, :, at], grad)
        add_to(div, at, dot_nn(low(probs), grad))
        inner = jnp.sum(probs * dprobs, axis=0, keepdims=True)
        dscores = low(probs * (dprobs - inner))
        add_to(dik, at, scale * dot_nn(dscores, tq[rows_t, at]))
        dtq[rows_t, at] = low(scale * dot_tn(dscores, ik[image, :, at]))


def backward_kernel(owner, *refs):
    shared = (owner,) + refs
    for ref in refs[10:13]:
        ref[...] = jnp.zeros_like(ref)

    def one(p, carry):
        attention_back_pair(p, shared)
        return carry

    lax.fori_loop(0, owner.shape[0], one, 0)


def backward_attention(owner, kept, dic, dtc):
    iq, ik, iv, tq, tk, tv, iprob, tprob = kept
    bf, f32 = jnp.bfloat16, jnp.float32
    shapes = [jax.ShapeDtypeStruct(iq.shape, f32)] * 3 + [jax.ShapeDtypeStruct(tq.shape, bf)] * 3
    return pl.pallas_call(
        backward_kernel,
        out_shape=shapes,
        in_specs=[SCALARS] + [WHOLE] * 10,
        out_specs=[WHOLE] * 6,
        compiler_params=pltpu.CompilerParams(vmem_limit_bytes=VMEM_LIMIT),
    )(owner, iq, ik, iv, tq, tk, tv, iprob, tprob, dic, dtc)


def data_grad_kernel(base, dq, dk, dv, wq, wk, wv, out):
    total = base[...]
    for d, w in ((dq, wq), (dk, wk), (dv, wv)):
        total = total + times_back(d[...], w)
    out[...] = total


def data_grad(base, grads, weights, block):
    rows, wide = base.shape
    bi = grads[0].shape[1]
    return pl.pallas_call(
        data_grad_kernel,
        grid=(rows // block,),
        in_specs=[pl.BlockSpec((block, wide), lambda i: (i, 0))]
        + [pl.BlockSpec((block, bi), lambda i: (i, 0))] * 3
        + [
            pl.BlockSpec(w.shape, lambda i: (0, 0, 0), pipeline_mode=pl.Buffered(1))
            for w in weights
        ],
        out_specs=pl.BlockSpec((block, wide), lambda i: (i, 0)),
        out_shape=jax.ShapeDtypeStruct((rows, wide), jnp.float32),
        compiler_params=pltpu.CompilerParams(vmem_limit_bytes=VMEM_LIMIT),
    )(base, *grads, *weights)


PARTS = (0, 1, 2, 0, 1, 2, 2, 0, 2, 1, 0, 1)


def mesh_bits():
    return bits_of(lax.axis_size("dp")), bits_of(lax.axis_size("fsdp"))


def gather_weights(shards, norm_params):
    nd, nf = mesh_bits()
    wide = norm_params.shape[1]
    padded = jnp.pad(norm_params, ((0, 8 - norm_params.shape[0]), (0, 128 - wide)))
    blocks = gather_blocks(list(shards) + [padded], PARTS + (0,), nd, nf, 0)
    weights = []
    for shard, block in zip(shards, blocks):
        rows, cols = shard.shape
        block = block.reshape(1 << nf, rows << nd, cols)
        if cols % 128:
            block = jnp.swapaxes(block, 0, 1).reshape(1, rows << nd, cols << nf)
        weights.append(block)
    norms = blocks[-1].reshape(1 << nf, 1 << nd, 8, 128)[:, :, :4, :wide]
    norms = norms.transpose(2, 1, 0, 3).reshape(4, wide << (nd + nf))
    return tuple(weights), norms


def reduce_grads(grads, shards, norm_rows):
    nd, nf = mesh_bits()
    lead = (2,) * (nd + nf)
    blocks = []
    for grad, shard in zip(grads, shards):
        rows, cols = shard.shape
        if cols % 128:
            grad = jnp.swapaxes(grad.reshape(rows << nd, 1 << nf, cols), 0, 1)
        blocks.append(grad.reshape(lead + (rows, cols)))
    wide = norm_rows.shape[1] >> (nd + nf)
    split = norm_rows.reshape(4, 1 << nd, 1 << nf, wide).transpose(2, 1, 0, 3)
    split = jnp.pad(split, ((0, 0), (0, 0), (0, 4), (0, 128 - wide)))
    blocks.append(split.reshape(lead + (8, 128)))
    owned = reduce_blocks(blocks, PARTS + (0,), nd, nf, 1)
    return tuple(owned[:-1]), owned[-1][:4, :wide]


def body(
    text_states,
    image_states,
    text_lengths,
    region_mask,
    group_ids,
    image_query,
    image_key,
    image_value,
    text_query,
    text_key,
    text_value,
    image_output,
    text_output,
    image_inner,
    image_outer,
    text_inner,
    text_outer,
    norm_params,
    cot_text,
    cot_image,
):
    shards = (
        image_query,
        image_key,
        image_value,
        text_query,
        text_key,
        text_value,
        image_output,
        text_output,
        image_inner,
        image_outer,
        text_inner,
        text_outer,
    )
    weights, norms = gather_weights(shards, norm_params)
    device = lax.axis_index("dp") * lax.axis_size("fsdp") + lax.axis_index("fsdp")
    results, grads, norm_rows = layer(
        text_states,
        image_states,
        text_lengths,
        region_mask,
        group_ids - device * image_states.shape[0],
        weights,
        norms,
        cot_text,
        cot_image,
    )
    owned, norm_grad = reduce_grads(grads, shards, norm_rows)
    return results + owned + (norm_grad,)


def layer(
    text_states, image_states, text_lengths, region_mask, owner, weights, norms, cot_text, cot_image
):
    pairs, length, width_text = text_states.shape
    images, regions, width_image = image_states.shape
    padded = -(-regions // 16) * 16
    extra = ((0, 0), (0, padded - regions), (0, 0))
    (
        query_image,
        key_image,
        value_image,
        query_text,
        key_text,
        value_text,
        out_image,
        out_text,
        inner_image,
        outer_image,
        inner_text,
        outer_text,
    ) = weights
    region_counts = jnp.sum(region_mask, axis=1)
    mine = owner[:, None] == jnp.arange(images, dtype=jnp.int32)[None, :]
    counts = jnp.sum(jnp.where(mine, region_counts[None, :], 0), axis=1)
    text = text_states.reshape(pairs * length, width_text)
    image = jnp.pad(image_states, extra)
    visual = image[0]
    for i in range(1, images):
        visual = jnp.where(mine[:, i, None, None], image[i], visual)
    visual = visual.reshape(pairs * padded, width_image)
    image = image.reshape(images * padded, width_image)
    cot_rows = jnp.pad(cot_image, extra).reshape(pairs * padded, width_image)

    def keep_rows(limits, slots):
        kept = jnp.arange(slots, dtype=jnp.int32)[None, :] < limits[:, None]
        return kept.astype(jnp.float32).reshape(-1, 1)

    *kept, image_context, text_context = forward_attention(
        text_lengths, owner, counts, text, image, weights[:6], images
    )
    (
        text_out,
        text_dz,
        text_mid,
        text_act,
        text_hid,
        text_ffn,
        text_branch,
        text_dctx,
        text_ngrad,
    ) = stream(
        text,
        text_context,
        cot_text.reshape(text.shape),
        keep_rows(text_lengths, length),
        norms[:, :width_text],
        out_text,
        inner_text,
        outer_text,
        256,
    )
    (
        image_out,
        image_dz,
        image_mid,
        image_act,
        image_hid,
        image_ffn,
        image_branch,
        image_dctx,
        image_ngrad,
    ) = stream(
        visual,
        image_context,
        cot_rows,
        keep_rows(counts, padded),
        norms[:, width_text:],
        out_image,
        inner_image,
        outer_image,
        pairs * padded // 2,
    )
    diq, dik, div, dtq, dtk, dtv = backward_attention(owner, kept, image_dctx, text_dctx)
    diq, dik, div = (low(d).reshape(image.shape[0], -1) for d in (diq, dik, div))
    text_grad = data_grad(text_dz, (dtq, dtk, dtv), weights[3:6], 256)
    by_pair = image_dz.reshape(pairs, padded, width_image)
    base = jnp.stack(
        [jnp.sum(jnp.where(mine[:, i, None, None], by_pair, 0.0), axis=0) for i in range(images)]
    )
    image_grad = data_grad(
        base.reshape(image.shape), (diq, dik, div), weights[:3], image.shape[0]
    )
    grads = []
    for x, d, w in (
        (image, diq, query_image),
        (image, dik, key_image),
        (image, div, value_image),
        (text, dtq, query_text),
        (text, dtk, key_text),
        (text, dtv, value_text),
        (image_context, image_branch, out_image),
        (text_context, text_branch, out_text),
        (image_mid, image_hid, inner_image),
        (image_act, image_ffn, outer_image),
        (text_mid, text_hid, inner_text),
        (text_act, text_ffn, outer_text),
    ):
        grads.append(weight_grad(x, d, w.shape[0]))
    norm_rows = jnp.concatenate([text_ngrad, image_ngrad], axis=1)
    results = (
        text_out.reshape(text_states.shape),
        image_out.reshape(pairs, padded, width_image)[:, :regions],
        text_grad.reshape(text_states.shape),
        image_grad.reshape(images, padded, width_image)[:, :regions],
    )
    return results, tuple(grads), norm_rows


def solution(mesh):
    placed = (
        P(("dp", "fsdp"), None, None),
        P(("dp", "fsdp"), None, None),
        P(("dp", "fsdp")),
        P(("dp", "fsdp"), None),
        P(("dp", "fsdp")),
        P("dp", "fsdp"),
        P("dp", "fsdp"),
        P("dp", "fsdp"),
        P("dp", "fsdp"),
        P("dp", "fsdp"),
        P("dp", "fsdp"),
        P("dp", "fsdp"),
        P("dp", "fsdp"),
        P("dp", "fsdp"),
        P("dp", "fsdp"),
        P("dp", "fsdp"),
        P("dp", "fsdp"),
        P(None, ("dp", "fsdp")),
        P(("dp", "fsdp"), None, None),
        P(("dp", "fsdp"), None, None),
    )
    return jax.shard_map(
        body,
        mesh=mesh,
        in_specs=placed,
        out_specs=(
            P(("dp", "fsdp"), None, None),
            P(("dp", "fsdp"), None, None),
            P(("dp", "fsdp"), None, None),
            P(("dp", "fsdp"), None, None),
            P("dp", "fsdp"),
            P("dp", "fsdp"),
            P("dp", "fsdp"),
            P("dp", "fsdp"),
            P("dp", "fsdp"),
            P("dp", "fsdp"),
            P("dp", "fsdp"),
            P("dp", "fsdp"),
            P("dp", "fsdp"),
            P("dp", "fsdp"),
            P("dp", "fsdp"),
            P("dp", "fsdp"),
            P(None, ("dp", "fsdp")),
        ),
        check_vma=False,
    )
```

time: 755 us -> 562 us (0.74)
  Pallas kernels: 278 us -> 523 us
  matrix products: 201 us -> 0 us
  local copies, waits for them, and re-layouts: 218 us -> 30.2 us
  other arithmetic: 50.1 us -> 6.41 us
    pallas_call x0 -> x18, Pallas kernels: none -> 245 us  [the longest x12 78.7 us: weight_grad(): pl.pallas_call(weight_grad_kernel, grid=(splits, inner // block), in_spec...]
    dot_general x49 -> x0, matrix products: 201 us -> none  [the longest x12 65.1 us: project_back(): jnp.einsum('bto,io->bti', grads, matrix, preferred_element_type=jnp.float32)]
    reshape x32 -> x3, local copies, waits for them, and re-layouts: 102 us -> 0.34 us  [the longest x2 0.2 us: reduce_grads(): split = norm_rows.reshape(4, 1 << nd, 1 << nf, wide).transpose(2, 1, 0, 3)]
    transpose x12 -> x0, local copies, waits for them, and re-layouts: 83.5 us -> none  [gather_weights(): weights.append(jnp.swapaxes(block, 0, 1).reshape(rows << nd, cols << nf))]
    convert_element_type x5, other arithmetic: 34.5 us -> 2.26 us  [the longest x3 2.12 us: low(): return value.astype(jnp.bfloat16)]
    reduce_sum x8 -> x3, other arithmetic: 12.5 us -> 1.68 us  [the longest x1 0.8 us: layer(): region_counts = jnp.sum(region_mask, axis=1)]
    unnamed x207 -> x47, local copies, waits for them, and re-layouts: 21.6 us -> 19.5 us
where the time goes in v2:
time: 562 us; the launch traced here: 560 us
  Pallas kernels  523 us (93%)
  local copies, waits for them, and re-layouts  30.2 us (5%)
  other arithmetic  6.41 us (1%)
    pallas_call x1, Pallas kernels, gather_blocks(): pl.pallas_call(functools.partial(gather_kernel, nd, nf, routes), out_shap...  144 us
    pallas_call x1, Pallas kernels, reduce_blocks(): pl.pallas_call(functools.partial(reduce_kernel, nd, nf, routes), out_shap...  133 us
    pallas_call x12, Pallas kernels, weight_grad(): pl.pallas_call(weight_grad_kernel, grid=(splits, inner // block), in_spec...  78.7 us
    pallas_call x2, Pallas kernels, stream(): pl.pallas_call(stream_kernel, grid=(rows // block,), in_specs=[by_row(wid...  68.2 us
    pallas_call x1, Pallas kernels, forward_attention(): pl.pallas_call(forward_kernel, out_shape=shapes, in_specs=[SCALARS] * 3 +...  45.8 us
    pallas_call x1, Pallas kernels, backward_attention(): pl.pallas_call(backward_kernel, out_shape=shapes, in_specs=[SCALARS] + [W...  35.6 us
    unnamed x47, local copies, waits for them, and re-layouts  19.5 us
    pallas_call x2, Pallas kernels, data_grad(): pl.pallas_call(data_grad_kernel, grid=(rows // block,), in_specs=[pl.Bloc...  16.6 us

profile of v2, /device:TPU:0, one launch (start us, length us, event | category | flops | bytes accessed | tf_op | source)
XLA Modules:
  0.0 560.0 jit_solution(12346027662941729399)
XLA Ops:
  1.3 0.8 reduce_sum.36
  2.7 0.9 copy.43
  3.7 0.7 pad.16
  4.4 1.3 pad.17.refs_12_
  5.6 144.2 %shard_map.323 = (bf16[2,2,2,2,2,64,512]{6,5,4,3,2,1,0:T(8,128)(2,1)}, bf16[2,2,2,2,2,64,512]{6,5,4,3,2,1,0:T(8,128)(2,1)}, bf16[2,2,2,2,2,64,512]{6,5,4,3,2,1,0...) custom-call(bf16[64,512]{1,0:T(8,128)(2,1)} %refs_0_.1, ...), custom_call_target="tpu_custom_call" | custom-call | tf_op jit(solution)/shard_map/pallas_call | solution.py:119
  149.9 45.8 %shard_map.324 = (bf16[2,48,1024]{2,1,0:T(8,128)(2,1)}, bf16[2,48,1024]{2,1,0:T(8,128)(2,1)}, bf16[2,48,1024]{2,1,0:T(8,128)(2,1)}, bf16[1024,1024]{1,0:T(8,128)...) custom-call(s32[8]{0:T(128)} %lens.1, ...), custom_call_target="tpu_custom_call" | custom-call | tf_op jit(solution)/shard_map/pallas_call | solution.py:354
  195.8 1.0 copy.45.keep
  197.6 52.5 %shard_map.325 = (bf16[1024,768]{1,0:T(8,128)(2,1)}, f32[1024,768]{1,0:T(8,128)}, bf16[1024,768]{1,0:T(8,128)(2,1)}, bf16[1024,3072]{1,0:T(8,128)(2,1)}, bf16[10...) custom-call(bf16[1024,768]{1,0:T(8,128)(2,1)} %bitcast.61, ...), custom_call_target="tpu_custom_call" | custom-call | tf_op jit(solution)/shard_map/pallas_call | solution.py:455
  250.4 1.0 bitcast_select_fusion.x
  251.7 1.0 pad.18.clone
  252.8 0.8 reshape.266.keep
  254.2 15.6 %shard_map.326 = (bf16[384,1024]{1,0:T(8,128)(2,1)}, f32[384,1024]{1,0:T(8,128)}, bf16[384,1024]{1,0:T(8,128)(2,1)}, bf16[384,1024]{1,0:T(8,128)(2,1)}, bf16[384...) custom-call(bf16[384,1024]{1,0:T(8,128)(2,1)} %bitcast_select_fusion, ...), custom_call_target="tpu_custom_call" | custom-call | tf_op jit(solution)/shard_map/pallas_call | solution.py:455
  269.9 1.1 slice.44
  271.0 1.1 copy.52
  272.1 35.6 %shard_map.327 = (f32[2,48,1024]{2,1,0:T(8,128)}, f32[2,48,1024]{2,1,0:T(8,128)}, f32[2,48,1024]{2,1,0:T(8,128)}, bf16[1024,1024]{1,0:T(8,128)(2,1)}, bf16[1024,...) custom-call(s32[8]{0:T(128)} %copy-done.11, bf16[2,48,1024]{2,1,0:T(8,128)(2,1)} %get-tuple-element.95.refs_0_, ...), custom_call_target="tpu_custom_call" | custom-call | tf_op jit(solution)/shard_map/pallas_call | solution.py:542
  307.7 10.5 %shard_map.328 = f32[1024,768]{1,0:T(8,128)} custom-call(f32[1024,768]{1,0:T(8,128)} %get-tuple-element.94.base, bf16[1024,1024]{1,0:T(8,128)(2,1)} %get-tuple-element.105.dq.d, bf16[1024,1024]{1,0:T(8,128)(2,1)} %get-tuple-element.106.dk.d, bf16[1024,1024]{1,0:T(8,128)(2,1)} %get-tuple-element.107.dv.d, bf16[2,768,512]{2,1,0:T(8,128)(2,1)} %bitcast.84, ...), custom_call_target="tpu_custom_call" | custom-call | tf_op jit(solution)/shard_map/pallas_call | solution.py:561
  318.6 0.8 pad_maximum_fusion
  319.3 0.7 convert_element_type.47
  320.1 0.7 convert_element_type.48
  320.8 0.7 convert_element_type.49
  321.5 6.0 %shard_map.329 = f32[96,1024]{1,0:T(8,128)} custom-call(f32[96,1024]{1,0:T(8,128)} %bitcast.109, bf16[96,1024]{1,0:T(8,128)(2,1)} %bitcast.100, bf16[96,1024]{1,0:T(8,128)(2,1)} %bitcast.102, bf16[96,1024]{1,0:T(8,128)(2,1)} %bitcast.104, bf16[2,1024,512]{2,1,0:T(8,128)(2,1)} %bitcast.74, bf16[2,1024,512]{2,1,0:T(8,128)(2,1)} %bitcast.76, ...), custom_call_target="tpu_custom_call" | custom-call | tf_op jit(solution)/shard_map/pallas_call | solution.py:561
  327.5 1.0 slice.45
  328.5 0.9 copy.53
  329.4 4.1 shard_map.330
  333.5 4.1 shard_map.331
  337.6 4.1 shard_map.332
  341.7 6.9 %shard_map.333 = bf16[2,768,512]{2,1,0:T(8,128)(2,1)} custom-call(bf16[1024,768]{1,0:T(8,128)(2,1)} %bitcast.62, bf16[1024,1024]{1,0:T(8,128)(2,1)} %get-tuple-element.105.dq.d), custom_call_target="tpu_custom_call" | custom-call | tf_op jit(solution)/shard_map/pallas_call | solution.py:477
  348.6 6.8 %shard_map.334 = bf16[2,768,512]{2,1,0:T(8,128)(2,1)} custom-call(bf16[1024,768]{1,0:T(8,128)(2,1)} %bitcast.63, bf16[1024,1024]{1,0:T(8,128)(2,1)} %get-tuple-element.106.dk.d), custom_call_target="tpu_custom_call" | custom-call | tf_op jit(solution)/shard_map/pallas_call | solution.py:477
  355.4 6.9 %shard_map.335 = bf16[2,768,512]{2,1,0:T(8,128)(2,1)} custom-call(bf16[1024,768]{1,0:T(8,128)(2,1)} %bitcast.64, bf16[1024,1024]{1,0:T(8,128)(2,1)} %get-tuple-element.107.dv.d), custom_call_target="tpu_custom_call" | custom-call | tf_op jit(solution)/shard_map/pallas_call | solution.py:477
  362.3 4.7 shard_map.336
  367.0 6.1 %shard_map.337 = bf16[2,1024,384]{2,1,0:T(8,128)(2,1)} custom-call(bf16[1024,1024]{1,0:T(8,128)(2,1)} %get-tuple-element.83.ctx.x, bf16[1024,768]{1,0:T(8,128)(2,1)} %get-tuple-element.113.d), custom_call_target="tpu_custom_call" | custom-call | tf_op jit(solution)/shard_map/pallas_call | solution.py:477
  373.1 4.7 shard_map.338
  377.8 4.7 shard_map.339
  382.5 10.9 %shard_map.340 = bf16[2,768,1536]{2,1,0:T(8,128)(2,1)} custom-call(bf16[1024,768]{1,0:T(8,128)(2,1)} %get-tuple-element.118.x, bf16[1024,3072]{1,0:T(8,128)(2,1)} %get-tuple-element.119.d), custom_call_target="tpu_custom_call" | custom-call | tf_op jit(solution)/shard_map/pallas_call | solution.py:477
  393.4 14.8 %shard_map.341 = bf16[2,3072,384]{2,1,0:T(8,128)(2,1)} custom-call(bf16[1024,3072]{1,0:T(8,128)(2,1)} %get-tuple-element.120.x, bf16[1024,768]{1,0:T(8,128)(2,1)} %get-tuple-element.121.d), custom_call_target="tpu_custom_call" | custom-call | tf_op jit(solution)/shard_map/pallas_call | solution.py:477
  409.1 133.5 %shard_map.342 = (f32[64,512]{1,0:T(8,128)}, f32[64,512]{1,0:T(8,128)}, f32[64,512]{1,0:T(8,128)}, f32[48,512]{1,0:T(8,128)}, f32[48,512]{1,0:T(8,128)}, /*index...) custom-call(bf16[2,2,2,2,2,64,512]{6,5,4,3,2,1,0:T(8,128)(2,1)} %bit, ...), custom_call_target="tpu_custom_call" | custom-call | tf_op jit(solution)/shard_map/pallas_call | solution.py:226
  542.6 1.3 slice.40
  543.9 1.6 copy.71
  545.5 1.6 copy.72
  547.1 1.6 copy.73
  548.6 1.5 copy.74
  550.2 1.5 copy.75
  551.7 1.5 copy.76
  553.3 1.6 copy.77
  554.8 1.5 copy.78
  556.4 1.6 copy.79
  558.6 0.7 copy.81
  559.3 0.7 copy.82
  (51 shorter events, 5.2 us)
Async XLA Ops:
  1.3 148.5 %copy-start.11 = (s32[8]{0:T(128)}, s32[8]{0:T(128)S(1)}, u32[]{:S(2)}) copy-start(s32[8]{0:T(128)S(1)} %broadcast_subtract_fusion.owner) | copy-start | bytes 100
  149.8 45.8 %copy-start.13 = (s32[8]{0:T(128)S(1)}, s32[8]{0:T(128)}, u32[]{:S(2)}) copy-start(s32[8]{0:T(128)} %lens.1) | copy-start | bytes 100
  149.9 46.9 %copy-start.8 = (f32[2,2,2,2,2,8,128]{6,5,4,3,2,1,0:T(8,128)S(1)}, f32[2,2,2,2,2,8,128]{6,5,4,3,2,1,0:T(8,128)}, u32[]{:S(2)}) copy-start(f32[2,2,2,2,2,8,128]{6,5,4,3,2,1,0:T(8,128)} %get-tuple-element.84) | copy-start | bytes 393220
  197.6 52.6 %copy-start.12 = (s32[8]{0:T(128)S(1)}, s32[8]{0:T(128)}, u32[]{:S(2)}) copy-start(s32[8]{0:T(128)} %copy-done.11) | copy-start | bytes 100
  197.6 53.8 %copy-start.1 = (bf16[8,36,1024]{2,0,1:T(8,128)(2,1)S(1)}, bf16[8,36,1024]{2,0,1:T(8,128)(2,1)}, u32[]{:S(2)}) copy-start(bf16[8,36,1024]{2,0,1:T(8,128)(2,1)} %param.39) | copy-start | bytes 1769476
  250.2 2.6 copy-start.14
  307.7 10.5 %copy-start = (f32[384,1024]{1,0:T(8,128)S(1)}, f32[384,1024]{1,0:T(8,128)}, u32[]{:S(2)}) copy-start(f32[384,1024]{1,0:T(8,128)} %get-tuple-element.108) | copy-start | bytes 4718596
  318.2 1.1 copy-start.4
  318.2 1.8 copy-start.3
  318.3 2.5 copy-start.2
  393.4 14.8 %copy-start.9 = (f32[4,1024]{1,0:T(4,128)S(1)}, f32[4,1024]{1,0:T(4,128)}, u32[]{:S(2)}) copy-start(f32[4,1024]{1,0:T(4,128)} %get-tuple-element.123) | copy-start | bytes 49156
  393.4 14.8 %copy-start.10 = (f32[4,768]{1,0:T(4,128)S(1)}, f32[4,768]{1,0:T(4,128)}, u32[]{:S(2)}) copy-start(f32[4,768]{1,0:T(4,128)} %get-tuple-element.122) | copy-start | bytes 36868
  542.6 15.4 %copy-start.7 = (f32[64,512]{1,0:T(8,128)S(1)}, f32[64,512]{1,0:T(8,128)}, u32[]{:S(2)}) copy-start(f32[64,512]{1,0:T(8,128)} %get-tuple-element.173) | copy-start | bytes 393220
  542.6 16.0 %copy-start.6 = (f32[48,1536]{1,0:T(8,128)S(1)}, f32[48,1536]{1,0:T(8,128)}, u32[]{:S(2)}) copy-start(f32[48,1536]{1,0:T(8,128)} %get-tuple-element.174) | copy-start | bytes 884740
  542.6 16.7 %copy-start.5 = (f32[192,384]{1,0:T(8,128)S(1)}, f32[192,384]{1,0:T(8,128)}, u32[]{:S(2)}) copy-start(f32[192,384]{1,0:T(8,128)} %get-tuple-element.175) | copy-start | bytes 884740
